TPU v7x, 32 devices: a whole 2x2x4 slice. The times are simulated.
32 devices in a mesh: row: 4 (over z), col: 8 (over y, x, core).
Axes of the slice: x: 2, y: 2, z: 4, core: 2. Of those that a mesh axis runs over, the one named last changes fastest.
Arguments:
- picture: float32 [3, 256, 1024], P(None, 'row', 'col'), may hold values from -6 to 6
- membrane: float32 [32, 128, 1024], P('row', 'col'), may hold values from -3 to 3
- dictionary: bfloat16 [1024, 3072], replicated, may hold values from -4 to 4
- momentum: float32 [1024, 3072], P(('row', 'col')), may hold values from -5 to 5
Outputs:
- final_codes: float32 [32, 128, 1024], P('row', 'col')
- new_dictionary: float32 [1024, 3072], P(('row', 'col'))
- new_momentum: float32 [1024, 3072], P(('row', 'col'))
All inputs are finite; a program needn't handle non-finite values.
Results may differ from a plain program's by a relative error of at most 0.0032.
Values may be sent and summed in bfloat16 or wider, within the bound.
No kernel may reach another device: no remote copies, remote signals or barrier semaphores. Data moves between devices by JAX's collectives and lax.ppermute only.
A program may use at most 64 MiB of HBM per device.

v0:
```python
import functools

import jax
import jax.numpy as jnp
from jax import lax
from jax.experimental import pallas as pl
from jax.experimental.pallas import tpu as pltpu
from jax.sharding import Mesh
from jax.sharding import PartitionSpec as P

PATCH_SIDE = 32
STRIDE = 8
SWEEPS = 2
SPAN = PATCH_SIDE // STRIDE
MARGIN = SPAN - 1

THRESHOLD = 0.25
RELAXATION = 0.1
DECAY = 0.9
LEARNING = 0.25
EPSILON = 1e-05

F32 = jnp.float32
BF16 = jnp.bfloat16
VMEM = pl.BlockSpec(memory_space=pltpu.VMEM)
SMEM = pl.BlockSpec(memory_space=pltpu.SMEM)
HBM = pl.BlockSpec(memory_space=pl.ANY)
PARAMS = pltpu.CompilerParams(vmem_limit_bytes=56 * 1024 * 1024)


def up_to(value, step):
    return -(-value // step) * step


def shrink(potential):
    return potential - jnp.clip(potential, -THRESHOLD, THRESHOLD)


def cells_of(picture):
    channels, height, width_px = picture.shape
    blocked = picture.reshape(channels, height // STRIDE, STRIDE, width_px // STRIDE, STRIDE)
    return blocked.transpose(1, 3, 0, 2, 4).reshape(
        (height // STRIDE) * (width_px // STRIDE), channels * STRIDE * STRIDE
    )


class Sizes:
    def __init__(self, site_rows, site_cols, atoms, patch_len):
        self.rows, self.cols, self.atoms, self.patch = site_rows, site_cols, atoms, patch_len
        self.cell = patch_len // (SPAN * SPAN)
        self.band = SPAN * self.cell
        self.sites = site_rows * site_cols
        self.tall = site_rows + MARGIN
        self.wide = site_cols + MARGIN
        self.wide_pad = up_to(self.wide, 8)
        self.tall_pad = up_to(self.tall, 16)
        self.lanes = up_to(self.cell, 128)
        self.scale = patch_len ** (-0.5)


def dictionary_copies(source, target, sems, z):
    return [
        pltpu.make_async_copy(
            source.at[:, i * z.band : (i + 1) * z.band],
            target.at[:, i * z.band : (i + 1) * z.band],
            sems.at[i],
        )
        for i in range(SPAN)
    ]


def reconstruct(z, coding, dic, pixels, edges, tall_sum, own, left, right, ready=None):
    tall_sum[z.sites :, :] = jnp.zeros((z.tall * z.cols - z.sites, z.band), F32)
    for i in range(SPAN):
        if ready is not None:
            ready(i)
        placed = jnp.dot(
            coding, dic[:, i * z.band : (i + 1) * z.band], preferred_element_type=F32
        )
        start = i * z.cols
        if i == 0:
            tall_sum[0 : z.sites, :] = placed
        else:
            tall_sum[start : start + z.sites, :] += placed
    own[...] = jnp.zeros((z.tall, z.wide_pad, z.lanes), F32)
    own[0 : z.rows, 0 : z.cols, 0 : z.cell] = pixels[...].reshape(z.rows, z.cols, z.cell)
    for j in range(SPAN):
        part = tall_sum[:, j * z.cell : (j + 1) * z.cell].reshape(z.tall, z.cols, z.cell)
        own[:, j : j + z.cols, 0 : z.cell] -= part * z.scale

    @pl.when(edges[0] == 1)
    def _():
        own[z.rows :] = jnp.zeros((MARGIN, z.wide_pad, z.lanes), F32)

    @pl.when(edges[1] == 1)
    def _():
        own[:, z.cols :] = jnp.zeros((z.tall, z.wide_pad - z.cols, z.lanes), F32)

    for c in range(MARGIN):
        left[c, 0 : z.tall, :] = own[:, c, :]
        right[c, 0 : z.tall, :] = own[:, z.cols + c, :]


def first_kernel(z, edges, membrane, pixels, source, own, left, right, dic, tall_sum, sems):
    copies = dictionary_copies(source, dic, sems, z)
    for copy in copies:
        copy.start()
    coding = shrink(membrane[...]).astype(BF16)
    reconstruct(
        z, coding, dic, pixels, edges, tall_sum, own, left, right, lambda i: copies[i].wait()
    )


def side_kernel(z, own, from_left, from_right, joined, up, down):
    joined[...] = own[...]
    for c in range(MARGIN):
        joined[:, c, :] += from_left[c, 0 : z.tall, :]
        joined[:, z.cols + c, :] += from_right[c, 0 : z.tall, :]
    up[...] = joined[0:MARGIN]
    down[...] = joined[z.rows :]


def windows_of(z, whole, wide_part, first_row, row_stride):
    for j in range(SPAN):
        part = whole[:, j : j + z.cols, 0 : z.cell].astype(BF16)
        for p in range(z.tall):
            wide_part[
                pl.ds(p * row_stride + first_row, z.cols), j * z.cell : (j + 1) * z.cell
            ] = part[p]


def sweep_kernel(
    z, last, groups, edges, potential, joined, from_above, from_below, pixels, source, *rest
):
    if last:
        new_potential, own, left, right, shared, dic, tall_sum, whole, wide_part, sems = rest
    else:
        new_potential, own, left, right, dic, tall_sum, whole, wide_part, sems = rest
    copies = dictionary_copies(source, dic, sems, z)
    for copy in copies:
        copy.start()
    whole[...] = joined[...]
    whole[0:MARGIN] += from_above[...]
    whole[z.rows :] += from_below[...]
    windows_of(z, whole, wide_part, 0, z.cols)
    drive = None
    for i in range(SPAN):
        copies[i].wait()
        term = lax.dot_general(
            wide_part[i * z.cols : i * z.cols + z.sites, :],
            dic[:, i * z.band : (i + 1) * z.band],
            (((1,), (1,)), ((), ())),
            preferred_element_type=F32,
        )
        drive = term if drive is None else drive + term
    old = potential[...]
    updated = old + RELAXATION * (drive * z.scale + shrink(old) - old)
    active = shrink(updated)
    coding = active.astype(BF16)
    if last:
        new_potential[...] = active
        rows_n, cores_n, owned = groups
        span = z.atoms // rows_n
        src = lax.broadcasted_iota(jnp.int32, (span, span), 0)
        dst = lax.broadcasted_iota(jnp.int32, (span, span), 1)
        per_core = span // cores_n
        core, rem = dst // per_core, dst % per_core
        wanted = (rem // owned) * (owned * cores_n) + core * owned + rem % owned
        order = (src == wanted).astype(F32).astype(BF16)
        for r in range(rows_n):
            sorted_codes = jnp.dot(
                coding[:, r * span : (r + 1) * span], order, preferred_element_type=F32
            ).astype(BF16)
            for k in range(cores_n):
                shared[r * cores_n + k] = sorted_codes[:, k * per_core : (k + 1) * per_core]
    else:
        new_potential[...] = updated
    reconstruct(z, coding, dic, pixels, edges, tall_sum, own, left, right)


def pack_kernel(z, own, from_left, from_right, packed, joined):
    joined[...] = own[...]
    for c in range(MARGIN):
        joined[:, c, :] += from_left[c, 0 : z.tall, :]
        joined[:, z.cols + c, :] += from_right[c, 0 : z.tall, :]
    for p in range(z.tall):
        packed[p * z.cols : (p + 1) * z.cols, :] = joined[p, 0 : z.cols, :].astype(BF16)
    base = z.tall * z.cols
    packed[base:, :] = jnp.zeros((MARGIN * z.tall_pad, z.lanes), BF16)
    for c in range(MARGIN):
        start = base + c * z.tall_pad
        packed[start : start + z.tall, :] = joined[:, z.cols + c, :].astype(BF16)


def learn_kernel(z, groups, shared, packed, partial, whole, wide_part, codes):
    rows_n, cores_n, _ = groups
    members = rows_n * cores_n
    stride = members * z.cols
    base = z.tall * z.cols

    def unpack(d, low, high):
        main = packed[d, low * z.cols : high * z.cols, :].astype(F32)
        main = main.reshape(high - low, z.cols, z.lanes)
        side = [
            packed[d, base + c * z.tall_pad : base + (c + 1) * z.tall_pad, :].astype(F32)[low:high]
            for c in range(MARGIN)
        ]
        return main, side

    def add(d, low, high, at, first):
        main, side = unpack(d, low, high)
        n = high - low
        if first:
            whole[at : at + n, 0 : z.cols, :] = main
        else:
            whole[at : at + n, 0 : z.cols, :] += main
        for c in range(MARGIN):
            if first:
                whole[at : at + n, z.cols + c, :] = side[c]
            else:
                whole[at : at + n, z.cols + c, :] += side[c]

    for r in range(rows_n):
        for k in range(cores_n):
            d = r * cores_n + k
            add(d, 0, z.tall, 0, True)
            if r > 0:
                add(d - cores_n, z.rows, z.tall, 0, False)
            if r + 1 < rows_n:
                add(d + cores_n, 0, MARGIN, z.rows, False)
            windows_of(z, whole, wide_part, d * z.cols, stride)
            for i in range(z.rows):
                codes[i * stride + d * z.cols : i * stride + (d + 1) * z.cols, :] = shared[
                    d, i * z.cols : (i + 1) * z.cols, :
                ]
    count = z.rows * stride
    across = codes[...].astype(F32).T.astype(BF16)
    for i in range(SPAN):
        term = jnp.dot(
            across, wide_part[i * stride : i * stride + count, :], preferred_element_type=F32
        )
        partial[:, i * z.band : (i + 1) * z.band] = (term * z.scale).astype(BF16)


def finish_kernel(parts, momentum, atoms, new_dictionary, new_momentum):
    learning = parts[0].astype(F32)
    for i in range(1, parts.shape[0]):
        learning = learning + parts[i].astype(F32)
    momentum_out = DECAY * momentum[...] + learning
    new_momentum[...] = momentum_out
    weights = atoms[...].astype(F32) + LEARNING * momentum_out
    power = jnp.mean(weights * weights, axis=1, keepdims=True)
    new_dictionary[...] = weights * lax.rsqrt(power + EPSILON)


def call(kernel, outs, inputs, specs, scratch, name):
    return pl.pallas_call(
        kernel,
        out_shape=[jax.ShapeDtypeStruct(s, d) for s, d in outs],
        in_specs=specs,
        out_specs=[VMEM] * len(outs),
        scratch_shapes=scratch,
        compiler_params=PARAMS,
        name=name,
    )(*inputs)


def shards(picture, membrane, dictionary, momentum):
    site_rows, site_cols, atom_count = membrane.shape
    z = Sizes(site_rows, site_cols, atom_count, dictionary.shape[1])
    rows_n, yx_n, cores_n = (lax.axis_size(a) for a in ("row", "yx", "core"))
    cols_n = yx_n * cores_n
    owned = momentum.shape[0]
    groups = (rows_n, cores_n, owned)
    row_at = lax.axis_index("row")
    col_at = lax.axis_index(("yx", "core"))
    edges = jnp.stack([row_at == rows_n - 1, col_at == cols_n - 1]).astype(jnp.int32)
    pixels = cells_of(picture)

    def along(axis, n, block, distance):
        return lax.ppermute(
            block, axis, [(i - distance, i) for i in range(n) if 0 <= i - distance < n]
        )

    def sideways(left, right):
        return (
            along(("yx", "core"), cols_n, right, 1),
            along(("yx", "core"), cols_n, left, -1),
        )

    own_s = (z.tall, z.wide_pad, z.lanes)
    edge_s = (MARGIN, z.tall_pad, z.lanes)
    rim_s = (MARGIN, z.wide_pad, z.lanes)
    dic_v = pltpu.VMEM((atom_count, z.patch), BF16)
    tall_v = pltpu.VMEM((z.tall * z.cols, z.band), F32)
    whole_v = pltpu.VMEM(own_s, F32)
    wide_v = pltpu.VMEM((z.tall * z.cols, z.band), BF16)
    sems = pltpu.SemaphoreType.DMA((SPAN,))
    sides = [(own_s, F32), (edge_s, F32), (edge_s, F32)]

    potential = membrane.reshape(z.sites, atom_count)
    own, left, right = call(
        functools.partial(first_kernel, z),
        sides,
        (edges, potential, pixels, dictionary),
        [SMEM, VMEM, VMEM, HBM],
        [dic_v, tall_v, sems],
        "first",
    )
    for repeat in range(SWEEPS):
        last = repeat == SWEEPS - 1
        from_left, from_right = sideways(left, right)
        joined, up, down = call(
            functools.partial(side_kernel, z),
            [(own_s, F32), (rim_s, F32), (rim_s, F32)],
            (own, from_left, from_right),
            [VMEM] * 3,
            [],
            "side",
        )
        from_above = along("row", rows_n, down, 1)
        from_below = along("row", rows_n, up, -1)
        outs = [((z.sites, atom_count), F32)] + sides
        if last:
            members = rows_n * cores_n
            outs = outs + [((members, z.sites, atom_count // members), BF16)]
        results = call(
            functools.partial(sweep_kernel, z, last, groups),
            outs,
            (edges, potential, joined, from_above, from_below, pixels, dictionary),
            [SMEM, VMEM, VMEM, VMEM, VMEM, VMEM, HBM],
            [dic_v, tall_v, whole_v, wide_v, sems],
            "sweep",
        )
        potential, own, left, right = results[:4]
    final_codes = potential.reshape(membrane.shape)
    shared = results[4]
    members = rows_n * cores_n
    shared = lax.all_to_all(shared, ("row", "core"), 0, 0, tiled=True)
    from_left, from_right = sideways(left, right)
    packed_rows = z.tall * z.cols + MARGIN * z.tall_pad
    (packed,) = call(
        functools.partial(pack_kernel, z),
        [((packed_rows, z.lanes), BF16)],
        (own, from_left, from_right),
        [VMEM] * 3,
        [whole_v],
        "pack",
    )
    packed = lax.all_gather(packed, ("row", "core"), axis=0, tiled=False)
    (partial,) = call(
        functools.partial(learn_kernel, z, groups),
        [((atom_count // members, z.patch), BF16)],
        (shared, packed),
        [VMEM] * 2,
        [
            whole_v,
            pltpu.VMEM((z.tall * members * z.cols, z.band), BF16),
            pltpu.VMEM((members * z.sites, atom_count // members), BF16),
        ],
        "learn",
    )
    parts = lax.all_to_all(
        partial.reshape(yx_n, owned, z.patch), "yx", 0, 0, tiled=True
    )
    atoms = lax.dynamic_slice_in_dim(dictionary, (row_at * cols_n + col_at) * owned, owned, 0)
    new_dictionary, new_momentum = call(
        finish_kernel,
        [(momentum.shape, F32), (momentum.shape, F32)],
        (parts, momentum, atoms),
        [VMEM] * 3,
        [],
        "finish",
    )
    return (final_codes, new_dictionary, new_momentum)


def solution(mesh):
    rows_n, cols_n = (mesh.shape["row"], mesh.shape["col"])
    cores_n = 2 if cols_n % 2 == 0 else 1
    split = Mesh(
        mesh.devices.reshape(rows_n, cols_n // cores_n, cores_n), ("row", "yx", "core")
    )
    col = ("yx", "core")
    return jax.shard_map(
        shards,
        mesh=split,
        in_specs=(P(None, "row", col), P("row", col, None), P(), P(("row",) + col, None)),
        out_specs=(P("row", col, None), P(("row",) + col, None), P(("row",) + col, None)),
        check_vma=False,
    )
```

profile of v0, /device:TPU:0, one launch (start us, length us, event | category | flops | bytes accessed | tf_op | source)
XLA Modules:
  0.0 126.6 jit_solution(12526339599664583051)
XLA Ops:
  0.6 1.7 %reshape.22 = f32[3,8,8,16,8]{4,3,2,1,0:T(8,128)S(1)} reshape(f32[3,64,128]{2,1,0:T(8,128)} %param.4) | data formatting | bytes 196608 | tf_op jit(solution)/shard_map/reshape | solution.py:41
  4.5 5.3 %first.1 = (f32[11,24,256]{2,1,0:T(8,128)}, f32[3,16,256]{2,1,0:T(8,128)}, f32[3,16,256]{2,1,0:T(8,128)}) custom-call(s32[2]{0:T(128)} %add_convert_fusion.edges, f32[128,1024]{1,0:T(8,128)} %bitcast.14, f32[128,192]{1,0:T(8,128)} %copy.9.pixels, bf16[1024,3072]{1,0:T(8,128)(2,1)} %source.5), custom_call_target="tpu_custom_call" | custom-call | tf_op jit(solution)/shard_map/first/pallas_call | solution.py:257
  9.7 2.4 %collective-permute-start = (f32[3,16,256]{2,1,0:T(8,128)}, f32[3,16,256]{2,1,0:T(8,128)S(1)}, u32[]{:S(2)}, u32[]{:S(2)}) collective-permute-start(f32[3,16,256]{2,1,0:T(8,128)} %get-tuple-element.24), channel_id=1, source_target_pairs={{0,1},{1,2},{2,3},{3,4},{4,5},{5,6},{6,7},{8,9},{9,10},{10,11},{11... | collective-permute-start | bytes 147464 | tf_op jit(solution)/shard_map/ppermute | solution.py:281
  12.2 1.3 %collective-permute-start.1 = (f32[3,16,256]{2,1,0:T(8,128)}, f32[3,16,256]{2,1,0:T(8,128)S(1)}, u32[]{:S(2)}, u32[]{:S(2)}) collective-permute-start(f32[3,16,256]{2,1,0:T(8,128)} %get-tuple-element.25), channel_id=1, source_target_pairs={{1,0},{2,1},{3,2},{4,3},{5,4},{6,5},{7,6},{9,8},{10,9},{11,10},{12... | collective-permute-start | bytes 147464 | tf_op jit(solution)/shard_map/ppermute | solution.py:281
  13.5 4.1 %collective-permute-done.1.from_right = f32[3,16,256]{2,1,0:T(8,128)S(1)} collective-permute-done((f32[3,16,256]{2,1,0:T(8,128)}, f32[3,16,256]{2,1,0:T(8,128)S(1)}, u32[]{:S(2)}, u32[]{:S(2)}) %collective-permute-start.1) | collective-permute-done | bytes 49184 | tf_op jit(solution)/shard_map/ppermute | solution.py:281
  18.2 1.8 %side.2 = (f32[11,24,256]{2,1,0:T(8,128)}, f32[3,24,256]{2,1,0:T(8,128)}, f32[3,24,256]{2,1,0:T(8,128)}) custom-call(f32[11,24,256]{2,1,0:T(8,128)} %get-tuple-element.23.own, f32[3,16,256]{2,1,0:T(8,128)} %copy-done.8, f32[3,16,256]{2,1,0:T(8,128)} %copy-done.10), custom_call_target="tpu_custom_call" | custom-call | tf_op jit(solution)/shard_map/side/pallas_call | solution.py:257
  20.0 3.5 %collective-permute-start.2 = (f32[3,24,256]{2,1,0:T(8,128)}, f32[3,24,256]{2,1,0:T(8,128)S(1)}, u32[]{:S(2)}, u32[]{:S(2)}) collective-permute-start(f32[3,24,256]{2,1,0:T(8,128)} %get-tuple-element.27), channel_id=1, source_target_pairs={{0,8},{8,16},{16,24},{1,9},{9,17},{17,25},{2,10},{10,18},{18,26},{... | collective-permute-start | bytes 221192 | tf_op jit(solution)/shard_map/ppermute | solution.py:281
  23.5 1.3 %collective-permute-start.3 = (f32[3,24,256]{2,1,0:T(8,128)}, f32[3,24,256]{2,1,0:T(8,128)S(1)}, u32[]{:S(2)}, u32[]{:S(2)}) collective-permute-start(f32[3,24,256]{2,1,0:T(8,128)} %get-tuple-element.28), channel_id=1, source_target_pairs={{8,0},{16,8},{24,16},{9,1},{17,9},{25,17},{10,2},{18,10},{26,18},{... | collective-permute-start | bytes 221192 | tf_op jit(solution)/shard_map/ppermute | solution.py:281
  24.8 1.0 collective-permute-done.2.from_above
  25.7 4.2 %collective-permute-done.3.from_below = f32[3,24,256]{2,1,0:T(8,128)S(1)} collective-permute-done((f32[3,24,256]{2,1,0:T(8,128)}, f32[3,24,256]{2,1,0:T(8,128)S(1)}, u32[]{:S(2)}, u32[]{:S(2)}) %collective-permute-start.3) | collective-permute-done | bytes 73760 | tf_op jit(solution)/shard_map/ppermute | solution.py:281
  30.6 7.8 %sweep.2 = (f32[128,1024]{1,0:T(8,128)}, f32[11,24,256]{2,1,0:T(8,128)}, f32[3,16,256]{2,1,0:T(8,128)}, f32[3,16,256]{2,1,0:T(8,128)}) custom-call(s32[2]{0:T(128)} %add_convert_fusion.edges, f32[128,1024]{1,0:T(8,128)} %bitcast.15, f32[11,24,256]{2,1,0:T(8,128)} %get-tuple-element.26.joined, f32[3,24,256]{2,1,0:T(8,128)} %copy-done.4, ...), custom_call_target="tpu_custom_call" | custom-call | tf_op jit(solution)/shard_map/sweep/pallas_call | solution.py:257
  38.3 3.3 %collective-permute-start.4 = (f32[3,16,256]{2,1,0:T(8,128)}, f32[3,16,256]{2,1,0:T(8,128)S(1)}, u32[]{:S(2)}, u32[]{:S(2)}) collective-permute-start(f32[3,16,256]{2,1,0:T(8,128)} %get-tuple-element.31), channel_id=1, source_target_pairs={{0,1},{1,2},{2,3},{3,4},{4,5},{5,6},{6,7},{8,9},{9,10},{10,11},{11... | collective-permute-start | bytes 147464 | tf_op jit(solution)/shard_map/ppermute | solution.py:281
  41.6 1.3 %collective-permute-start.5 = (f32[3,16,256]{2,1,0:T(8,128)}, f32[3,16,256]{2,1,0:T(8,128)S(1)}, u32[]{:S(2)}, u32[]{:S(2)}) collective-permute-start(f32[3,16,256]{2,1,0:T(8,128)} %get-tuple-element.32), channel_id=1, source_target_pairs={{1,0},{2,1},{3,2},{4,3},{5,4},{6,5},{7,6},{9,8},{10,9},{11,10},{12... | collective-permute-start | bytes 147464 | tf_op jit(solution)/shard_map/ppermute | solution.py:281
  42.9 3.0 %collective-permute-done.5.from_right = f32[3,16,256]{2,1,0:T(8,128)S(1)} collective-permute-done((f32[3,16,256]{2,1,0:T(8,128)}, f32[3,16,256]{2,1,0:T(8,128)S(1)}, u32[]{:S(2)}, u32[]{:S(2)}) %collective-permute-start.5) | collective-permute-done | bytes 49184 | tf_op jit(solution)/shard_map/ppermute | solution.py:281
  46.6 1.8 %side.3 = (f32[11,24,256]{2,1,0:T(8,128)}, f32[3,24,256]{2,1,0:T(8,128)}, f32[3,24,256]{2,1,0:T(8,128)}) custom-call(f32[11,24,256]{2,1,0:T(8,128)} %get-tuple-element.30.own, f32[3,16,256]{2,1,0:T(8,128)} %copy-done.9, f32[3,16,256]{2,1,0:T(8,128)} %copy-done.11), custom_call_target="tpu_custom_call" | custom-call | tf_op jit(solution)/shard_map/side/pallas_call | solution.py:257
  48.4 3.5 %collective-permute-start.6 = (f32[3,24,256]{2,1,0:T(8,128)}, f32[3,24,256]{2,1,0:T(8,128)S(1)}, u32[]{:S(2)}, u32[]{:S(2)}) collective-permute-start(f32[3,24,256]{2,1,0:T(8,128)} %get-tuple-element.34), channel_id=1, source_target_pairs={{0,8},{8,16},{16,24},{1,9},{9,17},{17,25},{2,10},{10,18},{18,26},{... | collective-permute-start | bytes 221192 | tf_op jit(solution)/shard_map/ppermute | solution.py:281
  51.8 1.3 %collective-permute-start.7 = (f32[3,24,256]{2,1,0:T(8,128)}, f32[3,24,256]{2,1,0:T(8,128)S(1)}, u32[]{:S(2)}, u32[]{:S(2)}) collective-permute-start(f32[3,24,256]{2,1,0:T(8,128)} %get-tuple-element.35), channel_id=1, source_target_pairs={{8,0},{16,8},{24,16},{9,1},{17,9},{25,17},{10,2},{18,10},{26,18},{... | collective-permute-start | bytes 221192 | tf_op jit(solution)/shard_map/ppermute | solution.py:281
  53.1 1.0 collective-permute-done.6.from_above
  54.1 4.2 %collective-permute-done.7.from_below = f32[3,24,256]{2,1,0:T(8,128)S(1)} collective-permute-done((f32[3,24,256]{2,1,0:T(8,128)}, f32[3,24,256]{2,1,0:T(8,128)S(1)}, u32[]{:S(2)}, u32[]{:S(2)}) %collective-permute-start.7) | collective-permute-done | bytes 73760 | tf_op jit(solution)/shard_map/ppermute | solution.py:281
  58.9 8.0 %sweep.3 = (f32[128,1024]{1,0:T(8,128)}, f32[11,24,256]{2,1,0:T(8,128)}, f32[3,16,256]{2,1,0:T(8,128)}, f32[3,16,256]{2,1,0:T(8,128)}, bf16[8,128,128]{2,1,0:T(8,128)(2,1)}) custom-call(s32[2]{0:T(128)} %add_convert_fusion.edges, f32[128,1024]{1,0:T(8,128)} %get-tuple-element.29.potential, f32[11,24,256]{2,1,0:T(8,128)} %get-tuple-element.33.joined, ...), custom_call_target="tpu_custom_call" | custom-call | tf_op jit(solution)/shard_map/sweep/pallas_call | solution.py:257
  66.9 3.8 %all-to-all-start = ((bf16[8,128,128]{2,1,0:T(8,128)(2,1)}), bf16[8,128,128]{2,1,0:T(8,128)(2,1)S(1)}, u32[]{:S(2)}, u32[]{:S(2)}) async-start(bf16[8,128,128]{2,1,0:T(8,128)(2,1)} %get-tuple-element.37), calls=%async_computation | async-start | bytes 524288 | tf_op jit(solution)/shard_map/all_to_all | solution.py:339
  70.7 2.8 %collective-permute-start.8 = (f32[3,16,256]{2,1,0:T(8,128)}, f32[3,16,256]{2,1,0:T(8,128)S(1)}, u32[]{:S(2)}, u32[]{:S(2)}) collective-permute-start(f32[3,16,256]{2,1,0:T(8,128)} %get-tuple-element.39), channel_id=1, source_target_pairs={{0,1},{1,2},{2,3},{3,4},{4,5},{5,6},{6,7},{8,9},{9,10},{10,11},{11... | collective-permute-start | bytes 147464 | tf_op jit(solution)/shard_map/ppermute | solution.py:281
  73.5 1.3 %collective-permute-start.9 = (f32[3,16,256]{2,1,0:T(8,128)}, f32[3,16,256]{2,1,0:T(8,128)S(1)}, u32[]{:S(2)}, u32[]{:S(2)}) collective-permute-start(f32[3,16,256]{2,1,0:T(8,128)} %get-tuple-element.40), channel_id=1, source_target_pairs={{1,0},{2,1},{3,2},{4,3},{5,4},{6,5},{7,6},{9,8},{10,9},{11,10},{12... | collective-permute-start | bytes 147464 | tf_op jit(solution)/shard_map/ppermute | solution.py:281
  74.8 4.2 %collective-permute-done.9.from_right = f32[3,16,256]{2,1,0:T(8,128)S(1)} collective-permute-done((f32[3,16,256]{2,1,0:T(8,128)}, f32[3,16,256]{2,1,0:T(8,128)S(1)}, u32[]{:S(2)}, u32[]{:S(2)}) %collective-permute-start.9) | collective-permute-done | bytes 49184 | tf_op jit(solution)/shard_map/ppermute | solution.py:281
  79.6 1.7 %pack.1 = bf16[224,256]{1,0:T(8,128)(2,1)} custom-call(f32[11,24,256]{2,1,0:T(8,128)} %get-tuple-element.38.own, f32[3,16,256]{2,1,0:T(8,128)} %copy-done.6, f32[3,16,256]{2,1,0:T(8,128)} %copy-done.7), custom_call_target="tpu_custom_call" | custom-call | tf_op jit(solution)/shard_map/pack/pallas_call | solution.py:257
  81.4 20.5 %all-gather = bf16[1792,256]{1,0:T(8,128)(2,1)} all-gather(bf16[224,256]{1,0:T(8,128)(2,1)} %pack.1), channel_id=2, replica_groups=mesh['row'=4,'yx'=4,'core'=2] {'row','core'}, dimensions={0}, use_global_device_ids=true | all-gather | bytes 1032192 | tf_op jit(solution)/shard_map/all_gather | solution.py:350
  102.5 4.3 %learn.1 = bf16[128,3072]{1,0:T(8,128)(2,1)} custom-call(bf16[8,128,128]{2,1,0:T(8,128)(2,1)} %copy-done.1, bf16[8,224,256]{2,1,0:T(8,128)(2,1)} %bitcast.12), custom_call_target="tpu_custom_call" | custom-call | tf_op jit(solution)/shard_map/learn/pallas_call | solution.py:257
  106.8 4.4 %all-to-all-start.1 = ((bf16[4,32,3072]{2,1,0:T(8,128)(2,1)}), bf16[4,32,3072]{2,1,0:T(8,128)(2,1)S(1)}, u32[]{:S(2)}, u32[]{:S(2)}) async-start(bf16[4,32,3072]{2,1,0:T(8,128)(2,1)} %bitcast.13), calls=%async_computation.1 | async-start | bytes 1572864 | tf_op jit(solution)/shard_map/all_to_all | solution.py:363
  111.3 1.6 %constant_dynamic-slice_fusion.atoms = bf16[32,3072]{1,0:T(8,128)(2,1)} fusion(bf16[1024,3072]{1,0:T(8,128)(2,1)} %source.5, s32[]{:T(128)S(6)} %select_n.3), kind=kLoop, calls=%fused_computation.1 | loop fusion | bytes 393220 | tf_op jit(solution)/shard_map/dynamic_slice | solution.py:366
  112.9 10.5 %all-to-all-done.1.parts = bf16[4,32,3072]{2,1,0:T(8,128)(2,1)S(1)} async-done(((bf16[4,32,3072]{2,1,0:T(8,128)(2,1)}), bf16[4,32,3072]{2,1,0:T(8,128)(2,1)S(1)}, u32[]{:S(2)}, u32[]{:S(2)}) %all-to-all-start.1) | async-done | bytes 786464 | tf_op jit(solution)/shard_map/all_to_all | solution.py:363
  123.4 0.9 copy-done
  124.2 2.3 %finish.1 = (f32[32,3072]{1,0:T(8,128)}, f32[32,3072]{1,0:T(8,128)}) custom-call(bf16[4,32,3072]{2,1,0:T(8,128)(2,1)} %copy-done, f32[32,3072]{1,0:T(8,128)} %momentum.1, bf16[32,3072]{1,0:T(8,128)(2,1)} %constant_dynamic-slice_fusion.atoms), custom_call_target="tpu_custom_call" | custom-call | tf_op jit(solution)/shard_map/finish/pallas_call | solution.py:257
  (31 shorter events, 5.9 us)
Async XLA Ops:
  9.7 3.7 %collective-permute-start = (f32[3,16,256]{2,1,0:T(8,128)}, f32[3,16,256]{2,1,0:T(8,128)S(1)}, u32[]{:S(2)}, u32[]{:S(2)}) collective-permute-start(f32[3,16,256]{2,1,0:T(8,128)} %get-tuple-element.24), channel_id=1, source_target_pairs={{0,1},{1,2},{2,3},{3,4},{4,5},{5,6},{6,7},{8,9},{9,10},{10,11},{11... | collective-permute-start | bytes 147464 | tf_op jit(solution)/shard_map/ppermute | solution.py:281
  12.2 5.4 %collective-permute-start.1 = (f32[3,16,256]{2,1,0:T(8,128)}, f32[3,16,256]{2,1,0:T(8,128)S(1)}, u32[]{:S(2)}, u32[]{:S(2)}) collective-permute-start(f32[3,16,256]{2,1,0:T(8,128)} %get-tuple-element.25), channel_id=1, source_target_pairs={{1,0},{2,1},{3,2},{4,3},{5,4},{6,5},{7,6},{9,8},{10,9},{11,10},{12... | collective-permute-start | bytes 147464 | tf_op jit(solution)/shard_map/ppermute | solution.py:281
  13.5 4.1 %copy-start.8 = (f32[3,16,256]{2,1,0:T(8,128)}, f32[3,16,256]{2,1,0:T(8,128)S(1)}, u32[]{:S(2)}) copy-start(f32[3,16,256]{2,1,0:T(8,128)S(1)} %collective-permute-done.from_left) | copy-start | bytes 147460
  17.6 0.6 copy-start.10
  20.0 5.8 %collective-permute-start.2 = (f32[3,24,256]{2,1,0:T(8,128)}, f32[3,24,256]{2,1,0:T(8,128)S(1)}, u32[]{:S(2)}, u32[]{:S(2)}) collective-permute-start(f32[3,24,256]{2,1,0:T(8,128)} %get-tuple-element.27), channel_id=1, source_target_pairs={{0,8},{8,16},{16,24},{1,9},{9,17},{17,25},{2,10},{10,18},{18,26},{... | collective-permute-start | bytes 221192 | tf_op jit(solution)/shard_map/ppermute | solution.py:281
  23.5 6.5 %collective-permute-start.3 = (f32[3,24,256]{2,1,0:T(8,128)}, f32[3,24,256]{2,1,0:T(8,128)S(1)}, u32[]{:S(2)}, u32[]{:S(2)}) collective-permute-start(f32[3,24,256]{2,1,0:T(8,128)} %get-tuple-element.28), channel_id=1, source_target_pairs={{8,0},{16,8},{24,16},{9,1},{17,9},{25,17},{10,2},{18,10},{26,18},{... | collective-permute-start | bytes 221192 | tf_op jit(solution)/shard_map/ppermute | solution.py:281
  25.7 4.2 %copy-start.4 = (f32[3,24,256]{2,1,0:T(8,128)}, f32[3,24,256]{2,1,0:T(8,128)S(1)}, u32[]{:S(2)}) copy-start(f32[3,24,256]{2,1,0:T(8,128)S(1)} %collective-permute-done.2.from_above) | copy-start | bytes 221188
  29.9 0.6 copy-start.5
  38.3 4.6 %collective-permute-start.4 = (f32[3,16,256]{2,1,0:T(8,128)}, f32[3,16,256]{2,1,0:T(8,128)S(1)}, u32[]{:S(2)}, u32[]{:S(2)}) collective-permute-start(f32[3,16,256]{2,1,0:T(8,128)} %get-tuple-element.31), channel_id=1, source_target_pairs={{0,1},{1,2},{2,3},{3,4},{4,5},{5,6},{6,7},{8,9},{9,10},{10,11},{11... | collective-permute-start | bytes 147464 | tf_op jit(solution)/shard_map/ppermute | solution.py:281
  41.6 4.4 %collective-permute-start.5 = (f32[3,16,256]{2,1,0:T(8,128)}, f32[3,16,256]{2,1,0:T(8,128)S(1)}, u32[]{:S(2)}, u32[]{:S(2)}) collective-permute-start(f32[3,16,256]{2,1,0:T(8,128)} %get-tuple-element.32), channel_id=1, source_target_pairs={{1,0},{2,1},{3,2},{4,3},{5,4},{6,5},{7,6},{9,8},{10,9},{11,10},{12... | collective-permute-start | bytes 147464 | tf_op jit(solution)/shard_map/ppermute | solution.py:281
  42.9 3.0 %copy-start.9 = (f32[3,16,256]{2,1,0:T(8,128)}, f32[3,16,256]{2,1,0:T(8,128)S(1)}, u32[]{:S(2)}) copy-start(f32[3,16,256]{2,1,0:T(8,128)S(1)} %collective-permute-done.4.from_left) | copy-start | bytes 147460
  46.0 0.6 copy-start.11
  48.4 5.8 %collective-permute-start.6 = (f32[3,24,256]{2,1,0:T(8,128)}, f32[3,24,256]{2,1,0:T(8,128)S(1)}, u32[]{:S(2)}, u32[]{:S(2)}) collective-permute-start(f32[3,24,256]{2,1,0:T(8,128)} %get-tuple-element.34), channel_id=1, source_target_pairs={{0,8},{8,16},{16,24},{1,9},{9,17},{17,25},{2,10},{10,18},{18,26},{... | collective-permute-start | bytes 221192 | tf_op jit(solution)/shard_map/ppermute | solution.py:281
  51.8 6.5 %collective-permute-start.7 = (f32[3,24,256]{2,1,0:T(8,128)}, f32[3,24,256]{2,1,0:T(8,128)S(1)}, u32[]{:S(2)}, u32[]{:S(2)}) collective-permute-start(f32[3,24,256]{2,1,0:T(8,128)} %get-tuple-element.35), channel_id=1, source_target_pairs={{8,0},{16,8},{24,16},{9,1},{17,9},{25,17},{10,2},{18,10},{26,18},{... | collective-permute-start | bytes 221192 | tf_op jit(solution)/shard_map/ppermute | solution.py:281
  54.1 4.2 %copy-start.2 = (f32[3,24,256]{2,1,0:T(8,128)}, f32[3,24,256]{2,1,0:T(8,128)S(1)}, u32[]{:S(2)}) copy-start(f32[3,24,256]{2,1,0:T(8,128)S(1)} %collective-permute-done.6.from_above) | copy-start | bytes 221188
  58.3 0.6 copy-start.3
  66.9 35.0 %all-to-all-start = ((bf16[8,128,128]{2,1,0:T(8,128)(2,1)}), bf16[8,128,128]{2,1,0:T(8,128)(2,1)S(1)}, u32[]{:S(2)}, u32[]{:S(2)}) async-start(bf16[8,128,128]{2,1,0:T(8,128)(2,1)} %get-tuple-element.37), calls=%async_computation | async-start | bytes 524288 | tf_op jit(solution)/shard_map/all_to_all | solution.py:339
  70.7 4.1 %collective-permute-start.8 = (f32[3,16,256]{2,1,0:T(8,128)}, f32[3,16,256]{2,1,0:T(8,128)S(1)}, u32[]{:S(2)}, u32[]{:S(2)}) collective-permute-start(f32[3,16,256]{2,1,0:T(8,128)} %get-tuple-element.39), channel_id=1, source_target_pairs={{0,1},{1,2},{2,3},{3,4},{4,5},{5,6},{6,7},{8,9},{9,10},{10,11},{11... | collective-permute-start | bytes 147464 | tf_op jit(solution)/shard_map/ppermute | solution.py:281
  73.5 5.5 %collective-permute-start.9 = (f32[3,16,256]{2,1,0:T(8,128)}, f32[3,16,256]{2,1,0:T(8,128)S(1)}, u32[]{:S(2)}, u32[]{:S(2)}) collective-permute-start(f32[3,16,256]{2,1,0:T(8,128)} %get-tuple-element.40), channel_id=1, source_target_pairs={{1,0},{2,1},{3,2},{4,3},{5,4},{6,5},{7,6},{9,8},{10,9},{11,10},{12... | collective-permute-start | bytes 147464 | tf_op jit(solution)/shard_map/ppermute | solution.py:281
  74.8 4.2 %copy-start.6 = (f32[3,16,256]{2,1,0:T(8,128)}, f32[3,16,256]{2,1,0:T(8,128)S(1)}, u32[]{:S(2)}) copy-start(f32[3,16,256]{2,1,0:T(8,128)S(1)} %collective-permute-done.8.from_left) | copy-start | bytes 147460
  79.0 0.6 copy-start.7
  101.8 0.7 copy-start.1
  106.8 16.5 %all-to-all-start.1 = ((bf16[4,32,3072]{2,1,0:T(8,128)(2,1)}), bf16[4,32,3072]{2,1,0:T(8,128)(2,1)S(1)}, u32[]{:S(2)}, u32[]{:S(2)}) async-start(bf16[4,32,3072]{2,1,0:T(8,128)(2,1)} %bitcast.13), calls=%async_computation.1 | async-start | bytes 1572864 | tf_op jit(solution)/shard_map/all_to_all | solution.py:363
  123.3 0.9 copy-start
where the time goes:
time: 127 us
  Pallas kernels  32.9 us (26%)
  waiting for transfers between devices  32.1 us (25%)
  starting transfers between devices  30.1 us (24%)
  blocking collectives  20.5 us (16%)
  local copies, waits for them, and re-layouts  9.56 us (8%)
    pallas_call x8, Pallas kernels, call(): pl.pallas_call(kernel, out_shape=[jax.ShapeDtypeStruct(s, d) for s, d in...  32.9 us
    ppermute x10, starting transfers between devices, along(): lax.ppermute(block, axis, [(i - distance, i) for i in range(n) if 0 <= i...  21.9 us
    ppermute x10, waiting for transfers between devices, along(): lax.ppermute(block, axis, [(i - distance, i) for i in range(n) if 0 <= i...  21.6 us
    all_gather x1, blocking collectives, shards(): packed = lax.all_gather(packed, ('row', 'core'), axis=0, tiled=False)  20.5 us
    all_to_all x1, waiting for transfers between devices, shards(): lax.all_to_all(partial.reshape(yx_n, owned, z.patch), 'yx', 0, 0, tiled=T...  10.5 us
    unnamed x24, local copies, waits for them, and re-layouts  4.7 us
    all_to_all x1, starting transfers between devices, shards(): lax.all_to_all(partial.reshape(yx_n, owned, z.patch), 'yx', 0, 0, tiled=T...  4.45 us
    all_to_all x1, starting transfers between devices, shards(): shared = lax.all_to_all(shared, ('row', 'core'), 0, 0, tiled=True)  3.82 us
  transfers between devices with their start and end apart: 12, of which 8 were waited for; matrix products, arithmetic and copies ran while one was open for 1% of the time, Pallas kernels for 1%

commit v1 on v0

--- a/solution.py
+++ b/solution.py
@@ -25,7 +25,7 @@
 VMEM = pl.BlockSpec(memory_space=pltpu.VMEM)
 SMEM = pl.BlockSpec(memory_space=pltpu.SMEM)
 HBM = pl.BlockSpec(memory_space=pl.ANY)
-PARAMS = pltpu.CompilerParams(vmem_limit_bytes=56 * 1024 * 1024)
+PARAMS = pltpu.CompilerParams(vmem_limit_bytes=24 * 1024 * 1024)
 
 
 def up_to(value, step):
@@ -34,14 +34,6 @@
 
 def shrink(potential):
     return potential - jnp.clip(potential, -THRESHOLD, THRESHOLD)
-
-
-def cells_of(picture):
-    channels, height, width_px = picture.shape
-    blocked = picture.reshape(channels, height // STRIDE, STRIDE, width_px // STRIDE, STRIDE)
-    return blocked.transpose(1, 3, 0, 2, 4).reshape(
-        (height // STRIDE) * (width_px // STRIDE), channels * STRIDE * STRIDE
-    )
 
 
 class Sizes:
@@ -101,10 +93,52 @@
         right[c, 0 : z.tall, :] = own[:, z.cols + c, :]
 
 
-def first_kernel(z, edges, membrane, pixels, source, own, left, right, dic, tall_sum, sems):
+def is_equal(a, b):
+    return (a == b).astype(F32).astype(BF16)
+
+
+def cells_of(z, picture, pixels, spread):
+    channels, height, width = picture.shape
+    flat = picture[...].reshape(channels * height, width)
+    high = flat.astype(BF16)
+    rest = flat - high.astype(F32)
+    middle = rest.astype(BF16)
+    low = (rest - middle.astype(F32)).astype(BF16)
+
+    def iota(shape, dim):
+        return lax.broadcasted_iota(jnp.int32, shape, dim)
+
+    shape = (channels * height, z.cell)
+    line = iota(shape, 0)
+    channel, image_row = line // height, line % height
+    entry = iota(shape, 1)
+    shape = (width, z.cell)
+    mine = (iota(shape, 0) % STRIDE == iota(shape, 1) % STRIDE).astype(F32)
+    for i in range(z.rows):
+        pick = is_equal(
+            (channel * STRIDE + image_row - i * STRIDE) * STRIDE + image_row // STRIDE * 65536,
+            entry // STRIDE * STRIDE + i * 65536,
+        )
+        for part, values in enumerate((high, middle, low)):
+            moved = lax.dot_general(
+                values, pick, (((0,), (0,)), ((), ())), preferred_element_type=F32
+            )
+            spread[part, i * width : (i + 1) * width, :] = (moved * mine).astype(BF16)
+    shape = (z.sites, z.rows * width)
+    gather = is_equal(iota(shape, 0), iota(shape, 1) // STRIDE)
+    parts = [
+        jnp.dot(gather, spread[part], preferred_element_type=F32) for part in range(3)
+    ]
+    pixels[...] = (parts[0] + parts[1]) + parts[2]
+
+
+def first_kernel(
+    z, edges, membrane, picture, source, own, left, right, pixels, dic, tall_sum, spread, sems
+):
     copies = dictionary_copies(source, dic, sems, z)
     for copy in copies:
         copy.start()
+    cells_of(z, picture, pixels, spread)
     coding = shrink(membrane[...]).astype(BF16)
     reconstruct(
         z, coding, dic, pixels, edges, tall_sum, own, left, right, lambda i: copies[i].wait()
@@ -130,22 +164,18 @@
 
 
 def sweep_kernel(
-    z, last, groups, edges, potential, joined, from_above, from_below, pixels, source, *rest
+    z, last, groups, edges, potential, joined, from_above, from_below, pixels, dic, *rest
 ):
     if last:
-        new_potential, own, left, right, shared, dic, tall_sum, whole, wide_part, sems = rest
+        new_potential, own, left, right, shared, tall_sum, whole, wide_part = rest
     else:
-        new_potential, own, left, right, dic, tall_sum, whole, wide_part, sems = rest
-    copies = dictionary_copies(source, dic, sems, z)
-    for copy in copies:
-        copy.start()
+        new_potential, own, left, right, tall_sum, whole, wide_part = rest
     whole[...] = joined[...]
     whole[0:MARGIN] += from_above[...]
     whole[z.rows :] += from_below[...]
     windows_of(z, whole, wide_part, 0, z.cols)
     drive = None
     for i in range(SPAN):
-        copies[i].wait()
         term = lax.dot_general(
             wide_part[i * z.cols : i * z.cols + z.sites, :],
             dic[:, i * z.band : (i + 1) * z.band],
@@ -166,7 +196,7 @@
         per_core = span // cores_n
         core, rem = dst // per_core, dst % per_core
         wanted = (rem // owned) * (owned * cores_n) + core * owned + rem % owned
-        order = (src == wanted).astype(F32).astype(BF16)
+        order = is_equal(src, wanted)
         for r in range(rows_n):
             sorted_codes = jnp.dot(
                 coding[:, r * span : (r + 1) * span], order, preferred_element_type=F32
@@ -256,13 +286,20 @@
 def call(kernel, outs, inputs, specs, scratch, name):
     return pl.pallas_call(
         kernel,
-        out_shape=[jax.ShapeDtypeStruct(s, d) for s, d in outs],
-        in_specs=specs,
+        out_shape=[
+            pltpu.VMEM(s, d) if kept else jax.ShapeDtypeStruct(s, d) for s, d, kept in outs
+        ],
+        in_specs=[spec or VMEM for spec in specs],
         out_specs=[VMEM] * len(outs),
         scratch_shapes=scratch,
         compiler_params=PARAMS,
         name=name,
-    )(*inputs)
+    )(
+        *(
+            x if spec else pltpu.with_memory_space_constraint(x, pltpu.VMEM)
+            for x, spec in zip(inputs, specs)
+        )
+    )
 
 
 def shards(picture, membrane, dictionary, momentum):
@@ -275,7 +312,6 @@
     row_at = lax.axis_index("row")
     col_at = lax.axis_index(("yx", "core"))
     edges = jnp.stack([row_at == rows_n - 1, col_at == cols_n - 1]).astype(jnp.int32)
-    pixels = cells_of(picture)
 
     def along(axis, n, block, distance):
         return lax.ppermute(
@@ -291,20 +327,20 @@
     own_s = (z.tall, z.wide_pad, z.lanes)
     edge_s = (MARGIN, z.tall_pad, z.lanes)
     rim_s = (MARGIN, z.wide_pad, z.lanes)
-    dic_v = pltpu.VMEM((atom_count, z.patch), BF16)
     tall_v = pltpu.VMEM((z.tall * z.cols, z.band), F32)
     whole_v = pltpu.VMEM(own_s, F32)
     wide_v = pltpu.VMEM((z.tall * z.cols, z.band), BF16)
     sems = pltpu.SemaphoreType.DMA((SPAN,))
-    sides = [(own_s, F32), (edge_s, F32), (edge_s, F32)]
+    sides = [(own_s, F32, True), (edge_s, F32, True), (edge_s, F32, True)]
 
     potential = membrane.reshape(z.sites, atom_count)
-    own, left, right = call(
+    spread_v = pltpu.VMEM((3, z.rows * picture.shape[2], z.cell), BF16)
+    own, left, right, pixels, dic = call(
         functools.partial(first_kernel, z),
-        sides,
-        (edges, potential, pixels, dictionary),
+        sides + [((z.sites, z.cell), F32, True), (dictionary.shape, BF16, True)],
+        (edges, potential, picture, dictionary),
         [SMEM, VMEM, VMEM, HBM],
-        [dic_v, tall_v, sems],
+        [tall_v, spread_v, sems],
         "first",
     )
     for repeat in range(SWEEPS):
@@ -312,24 +348,24 @@
         from_left, from_right = sideways(left, right)
         joined, up, down = call(
             functools.partial(side_kernel, z),
-            [(own_s, F32), (rim_s, F32), (rim_s, F32)],
+            [(own_s, F32, True), (rim_s, F32, True), (rim_s, F32, True)],
             (own, from_left, from_right),
-            [VMEM] * 3,
+            [None] * 3,
             [],
             "side",
         )
         from_above = along("row", rows_n, down, 1)
         from_below = along("row", rows_n, up, -1)
-        outs = [((z.sites, atom_count), F32)] + sides
+        outs = [((z.sites, atom_count), F32, not last)] + sides
         if last:
             members = rows_n * cores_n
-            outs = outs + [((members, z.sites, atom_count // members), BF16)]
+            outs = outs + [((members, z.sites, atom_count // members), BF16, True)]
         results = call(
             functools.partial(sweep_kernel, z, last, groups),
             outs,
-            (edges, potential, joined, from_above, from_below, pixels, dictionary),
-            [SMEM, VMEM, VMEM, VMEM, VMEM, VMEM, HBM],
-            [dic_v, tall_v, whole_v, wide_v, sems],
+            (edges, potential, joined, from_above, from_below, pixels, dic),
+            [SMEM, None if repeat else VMEM] + [None] * 5,
+            [tall_v, whole_v, wide_v],
             "sweep",
         )
         potential, own, left, right = results[:4]
@@ -341,18 +377,18 @@
     packed_rows = z.tall * z.cols + MARGIN * z.tall_pad
     (packed,) = call(
         functools.partial(pack_kernel, z),
-        [((packed_rows, z.lanes), BF16)],
+        [((packed_rows, z.lanes), BF16, True)],
         (own, from_left, from_right),
-        [VMEM] * 3,
+        [None] * 3,
         [whole_v],
         "pack",
     )
     packed = lax.all_gather(packed, ("row", "core"), axis=0, tiled=False)
     (partial,) = call(
         functools.partial(learn_kernel, z, groups),
-        [((atom_count // members, z.patch), BF16)],
+        [((atom_count // members, z.patch), BF16, True)],
         (shared, packed),
-        [VMEM] * 2,
+        [None] * 2,
         [
             whole_v,
             pltpu.VMEM((z.tall * members * z.cols, z.band), BF16),
@@ -366,9 +402,9 @@
     atoms = lax.dynamic_slice_in_dim(dictionary, (row_at * cols_n + col_at) * owned, owned, 0)
     new_dictionary, new_momentum = call(
         finish_kernel,
-        [(momentum.shape, F32), (momentum.shape, F32)],
+        [(momentum.shape, F32, False), (momentum.shape, F32, False)],
         (parts, momentum, atoms),
-        [VMEM] * 3,
+        [None, VMEM, VMEM],
         [],
         "finish",
     )

time: 127 us -> 107 us (0.84)
  Pallas kernels: 32.9 us -> 18.7 us
  local copies, waits for them, and re-layouts: 9.56 us -> 5.66 us
  blocking collectives: 20.5 us -> 19.2 us
    pallas_call x8, Pallas kernels: 32.9 us -> 18.7 us  [call(): pl.pallas_call(kernel, out_shape=[pltpu.VMEM(s, d) if kept else jax.Shape...]
    reshape x3 -> x0, local copies, waits for them, and re-layouts: 2.73 us -> none  [the longest x1 1.73 us: cells_of(): picture.reshape(channels, height // STRIDE, STRIDE, width_px // STRIDE, S...]
    all_gather x1, blocking collectives: 20.5 us -> 19.2 us  [shards(): packed = lax.all_gather(packed, ('row', 'core'), axis=0, tiled=False)]
    unnamed x24 -> x8, local copies, waits for them, and re-layouts: 4.7 us -> 4.72 us
  transfers between devices with their start and end apart: 12 -> 12, of which waited for: 8 -> 8; matrix products, arithmetic and copies ran while one was open for 1% -> 1% of each run, Pallas kernels for 1% -> 0%
where the time goes in v1:
time: 107 us; the launch traced here: 106 us
  waiting for transfers between devices  31.7 us (30%)
  starting transfers between devices  30.1 us (28%)
  blocking collectives  19.2 us (18%)
  Pallas kernels  18.7 us (17%)
  local copies, waits for them, and re-layouts  5.66 us (5%)
    ppermute x10, starting transfers between devices, along(): lax.ppermute(block, axis, [(i - distance, i) for i in range(n) if 0 <= i...  21.9 us
    ppermute x10, waiting for transfers between devices, along(): lax.ppermute(block, axis, [(i - distance, i) for i in range(n) if 0 <= i...  20.6 us
    all_gather x1, blocking collectives, shards(): packed = lax.all_gather(packed, ('row', 'core'), axis=0, tiled=False)  19.2 us
    pallas_call x8, Pallas kernels, call(): pl.pallas_call(kernel, out_shape=[pltpu.VMEM(s, d) if kept else jax.Shape...  18.7 us
    all_to_all x1, waiting for transfers between devices, shards(): lax.all_to_all(partial.reshape(yx_n, owned, z.patch), 'yx', 0, 0, tiled=T...  11.1 us
    unnamed x8, local copies, waits for them, and re-layouts  4.72 us
    all_to_all x1, starting transfers between devices, shards(): lax.all_to_all(partial.reshape(yx_n, owned, z.patch), 'yx', 0, 0, tiled=T...  4.34 us
    all_to_all x1, starting transfers between devices, shards(): shared = lax.all_to_all(shared, ('row', 'core'), 0, 0, tiled=True)  3.81 us
  transfers between devices with their start and end apart: 12, of which 8 were waited for; matrix products, arithmetic and copies ran while one was open for 1% of the time, Pallas kernels for 0%

profile of v1, /device:TPU:0, one launch (start us, length us, event | category | flops | bytes accessed | tf_op | source)
XLA Modules:
  0.0 106.2 jit_solution(5590678790520828655)
XLA Ops:
  0.7 2.8 %copy-done = bf16[1024,3072]{1,0:T(8,128)(2,1)S(1)} copy-done((bf16[1024,3072]{1,0:T(8,128)(2,1)S(1)}, bf16[1024,3072]{1,0:T(8,128)(2,1)}, u32[]{:S(2)}) %copy-start) | copy-done | bytes 6291480
  3.5 1.0 copy-done.1
  4.5 0.9 copy-done.3
  5.4 5.0 %first.1 = (f32[11,24,256]{2,1,0:T(8,128)S(1)}, f32[3,16,256]{2,1,0:T(8,128)S(1)}, f32[3,16,256]{2,1,0:T(8,128)S(1)}, f32[128,192]{1,0:T(8,128)S(1)}, bf16[1024,3072]{1,0:T(8,128)(2,1)S(1)}) custom-call(s32[2]{0:T(128)S(1)} %add_convert_fusion.edges, f32[128,1024]{1,0:T(8,128)S(1)} %bitcast.7, f32[3,64,128]{2,1,0:T(8,128)S(1)} %copy-done.3, ...), custom_call_target="tpu_custom_call" | custom-call | tf_op jit(solution)/shard_map/first/pallas_call | solution.py:287
  10.4 2.4 %collective-permute-start = (f32[3,16,256]{2,1,0:T(8,128)S(1)}, f32[3,16,256]{2,1,0:T(8,128)S(1)}, u32[]{:S(2)}, u32[]{:S(2)}) collective-permute-start(f32[3,16,256]{2,1,0:T(8,128)S(1)} %get-tuple-element.26), channel_id=1, source_target_pairs={{0,1},{1,2},{2,3},{3,4},{4,5},{5,6},{6,7},{8,9},{9,10},{10,11},{11... | collective-permute-start | bytes 147464 | tf_op jit(solution)/shard_map/ppermute | solution.py:317
  12.8 1.3 %collective-permute-start.1 = (f32[3,16,256]{2,1,0:T(8,128)S(1)}, f32[3,16,256]{2,1,0:T(8,128)S(1)}, u32[]{:S(2)}, u32[]{:S(2)}) collective-permute-start(f32[3,16,256]{2,1,0:T(8,128)S(1)} %get-tuple-element.27), channel_id=1, source_target_pairs={{1,0},{2,1},{3,2},{4,3},{5,4},{6,5},{7,6},{9,8},{10,9},{11,10},{12... | collective-permute-start | bytes 147464 | tf_op jit(solution)/shard_map/ppermute | solution.py:317
  14.1 3.9 %collective-permute-done.1.from_right = f32[3,16,256]{2,1,0:T(8,128)S(1)} collective-permute-done((f32[3,16,256]{2,1,0:T(8,128)S(1)}, f32[3,16,256]{2,1,0:T(8,128)S(1)}, u32[]{:S(2)}, u32[]{:S(2)}) %collective-permute-start.1) | collective-permute-done | bytes 49184 | tf_op jit(solution)/shard_map/ppermute | solution.py:317
  18.0 0.1 side.2
  18.1 3.5 %collective-permute-start.2 = (f32[3,24,256]{2,1,0:T(8,128)S(1)}, f32[3,24,256]{2,1,0:T(8,128)S(1)}, u32[]{:S(2)}, u32[]{:S(2)}) collective-permute-start(f32[3,24,256]{2,1,0:T(8,128)S(1)} %get-tuple-element.29), channel_id=1, source_target_pairs={{0,8},{8,16},{16,24},{1,9},{9,17},{17,25},{2,10},{10,18},{18,26},{... | collective-permute-start | bytes 221192 | tf_op jit(solution)/shard_map/ppermute | solution.py:317
  21.6 1.3 %collective-permute-start.3 = (f32[3,24,256]{2,1,0:T(8,128)S(1)}, f32[3,24,256]{2,1,0:T(8,128)S(1)}, u32[]{:S(2)}, u32[]{:S(2)}) collective-permute-start(f32[3,24,256]{2,1,0:T(8,128)S(1)} %get-tuple-element.30), channel_id=1, source_target_pairs={{8,0},{16,8},{24,16},{9,1},{17,9},{25,17},{10,2},{18,10},{26,18},{... | collective-permute-start | bytes 221192 | tf_op jit(solution)/shard_map/ppermute | solution.py:317
  22.9 0.7 collective-permute-done.2.from_above
  23.6 4.3 %collective-permute-done.3.from_below = f32[3,24,256]{2,1,0:T(8,128)S(1)} collective-permute-done((f32[3,24,256]{2,1,0:T(8,128)S(1)}, f32[3,24,256]{2,1,0:T(8,128)S(1)}, u32[]{:S(2)}, u32[]{:S(2)}) %collective-permute-start.3) | collective-permute-done | bytes 73760 | tf_op jit(solution)/shard_map/ppermute | solution.py:317
  27.9 4.2 %sweep.2 = (f32[128,1024]{1,0:T(8,128)S(1)}, f32[11,24,256]{2,1,0:T(8,128)S(1)}, f32[3,16,256]{2,1,0:T(8,128)S(1)}, f32[3,16,256]{2,1,0:T(8,128)S(1)}) custom-call(s32[2]{0:T(128)S(1)} %add_convert_fusion.edges, f32[128,1024]{1,0:T(8,128)S(1)} %bitcast.8, f32[11,24,256]{2,1,0:T(8,128)S(1)} %get-tuple-element.28.joined, ...), custom_call_target="tpu_custom_call" | custom-call | tf_op jit(solution)/shard_map/sweep/pallas_call | solution.py:287
  32.1 3.3 %collective-permute-start.4 = (f32[3,16,256]{2,1,0:T(8,128)S(1)}, f32[3,16,256]{2,1,0:T(8,128)S(1)}, u32[]{:S(2)}, u32[]{:S(2)}) collective-permute-start(f32[3,16,256]{2,1,0:T(8,128)S(1)} %get-tuple-element.35), channel_id=1, source_target_pairs={{0,1},{1,2},{2,3},{3,4},{4,5},{5,6},{6,7},{8,9},{9,10},{10,11},{11... | collective-permute-start | bytes 147464 | tf_op jit(solution)/shard_map/ppermute | solution.py:317
  35.4 1.3 %collective-permute-start.5 = (f32[3,16,256]{2,1,0:T(8,128)S(1)}, f32[3,16,256]{2,1,0:T(8,128)S(1)}, u32[]{:S(2)}, u32[]{:S(2)}) collective-permute-start(f32[3,16,256]{2,1,0:T(8,128)S(1)} %get-tuple-element.36), channel_id=1, source_target_pairs={{1,0},{2,1},{3,2},{4,3},{5,4},{6,5},{7,6},{9,8},{10,9},{11,10},{12... | collective-permute-start | bytes 147464 | tf_op jit(solution)/shard_map/ppermute | solution.py:317
  36.7 2.7 %collective-permute-done.5.from_right = f32[3,16,256]{2,1,0:T(8,128)S(1)} collective-permute-done((f32[3,16,256]{2,1,0:T(8,128)S(1)}, f32[3,16,256]{2,1,0:T(8,128)S(1)}, u32[]{:S(2)}, u32[]{:S(2)}) %collective-permute-start.5) | collective-permute-done | bytes 49184 | tf_op jit(solution)/shard_map/ppermute | solution.py:317
  39.5 3.5 %collective-permute-start.6 = (f32[3,24,256]{2,1,0:T(8,128)S(1)}, f32[3,24,256]{2,1,0:T(8,128)S(1)}, u32[]{:S(2)}, u32[]{:S(2)}) collective-permute-start(f32[3,24,256]{2,1,0:T(8,128)S(1)} %get-tuple-element.38), channel_id=1, source_target_pairs={{0,8},{8,16},{16,24},{1,9},{9,17},{17,25},{2,10},{10,18},{18,26},{... | collective-permute-start | bytes 221192 | tf_op jit(solution)/shard_map/ppermute | solution.py:317
  43.0 1.3 %collective-permute-start.7 = (f32[3,24,256]{2,1,0:T(8,128)S(1)}, f32[3,24,256]{2,1,0:T(8,128)S(1)}, u32[]{:S(2)}, u32[]{:S(2)}) collective-permute-start(f32[3,24,256]{2,1,0:T(8,128)S(1)} %get-tuple-element.39), channel_id=1, source_target_pairs={{8,0},{16,8},{24,16},{9,1},{17,9},{25,17},{10,2},{18,10},{26,18},{... | collective-permute-start | bytes 221192 | tf_op jit(solution)/shard_map/ppermute | solution.py:317
  44.3 0.7 collective-permute-done.6.from_above
  45.0 4.3 %collective-permute-done.7.from_below = f32[3,24,256]{2,1,0:T(8,128)S(1)} collective-permute-done((f32[3,24,256]{2,1,0:T(8,128)S(1)}, f32[3,24,256]{2,1,0:T(8,128)S(1)}, u32[]{:S(2)}, u32[]{:S(2)}) %collective-permute-start.7) | collective-permute-done | bytes 73760 | tf_op jit(solution)/shard_map/ppermute | solution.py:317
  49.3 5.1 %sweep.3 = (f32[128,1024]{1,0:T(8,128)}, f32[11,24,256]{2,1,0:T(8,128)S(1)}, f32[3,16,256]{2,1,0:T(8,128)S(1)}, f32[3,16,256]{2,1,0:T(8,128)S(1)}, bf16[8,128,128]{2,1,0:T(8,128)(2,1)}) custom-call(s32[2]{0:T(128)S(1)} %add_convert_fusion.edges, f32[128,1024]{1,0:T(8,128)S(1)} %get-tuple-element.33.potential, f32[11,24,256]{2,1,0:T(8,128)S(1)} %get-tuple-element.37.joined, ...), custom_call_target="tpu_custom_call" | custom-call | tf_op jit(solution)/shard_map/sweep/pallas_call | solution.py:287
  54.4 3.8 %all-to-all-start = ((bf16[8,128,128]{2,1,0:T(8,128)(2,1)}), bf16[8,128,128]{2,1,0:T(8,128)(2,1)S(1)}, u32[]{:S(2)}, u32[]{:S(2)}) async-start(bf16[8,128,128]{2,1,0:T(8,128)(2,1)} %get-tuple-element.41), calls=%async_computation | async-start | bytes 524288 | tf_op jit(solution)/shard_map/all_to_all | solution.py:375
  58.2 2.8 %collective-permute-start.8 = (f32[3,16,256]{2,1,0:T(8,128)S(1)}, f32[3,16,256]{2,1,0:T(8,128)S(1)}, u32[]{:S(2)}, u32[]{:S(2)}) collective-permute-start(f32[3,16,256]{2,1,0:T(8,128)S(1)} %get-tuple-element.43), channel_id=1, source_target_pairs={{0,1},{1,2},{2,3},{3,4},{4,5},{5,6},{6,7},{8,9},{9,10},{10,11},{11... | collective-permute-start | bytes 147464 | tf_op jit(solution)/shard_map/ppermute | solution.py:317
  61.0 1.3 %collective-permute-start.9 = (f32[3,16,256]{2,1,0:T(8,128)S(1)}, f32[3,16,256]{2,1,0:T(8,128)S(1)}, u32[]{:S(2)}, u32[]{:S(2)}) collective-permute-start(f32[3,16,256]{2,1,0:T(8,128)S(1)} %get-tuple-element.44), channel_id=1, source_target_pairs={{1,0},{2,1},{3,2},{4,3},{5,4},{6,5},{7,6},{9,8},{10,9},{11,10},{12... | collective-permute-start | bytes 147464 | tf_op jit(solution)/shard_map/ppermute | solution.py:317
  62.3 4.1 %collective-permute-done.9.from_right = f32[3,16,256]{2,1,0:T(8,128)S(1)} collective-permute-done((f32[3,16,256]{2,1,0:T(8,128)S(1)}, f32[3,16,256]{2,1,0:T(8,128)S(1)}, u32[]{:S(2)}, u32[]{:S(2)}) %collective-permute-start.9) | collective-permute-done | bytes 49184 | tf_op jit(solution)/shard_map/ppermute | solution.py:317
  66.4 0.1 pack.1
  66.5 19.2 %all-gather = bf16[1792,256]{1,0:T(8,128)(2,1)S(1)} all-gather(bf16[224,256]{1,0:T(8,128)(2,1)S(1)} %pack.1), channel_id=2, replica_groups=mesh['row'=4,'yx'=4,'core'=2] {'row','core'}, dimensions={0}, use_global_device_ids=true | all-gather | bytes 1032192 | tf_op jit(solution)/shard_map/all_gather | solution.py:386
  85.7 3.0 %learn.1 = bf16[128,3072]{1,0:T(8,128)(2,1)} custom-call(bf16[8,128,128]{2,1,0:T(8,128)(2,1)S(1)} %all-to-all-done.shared, bf16[8,224,256]{2,1,0:T(8,128)(2,1)S(1)} %bitcast.6), custom_call_target="tpu_custom_call" | custom-call | tf_op jit(solution)/shard_map/learn/pallas_call | solution.py:287
  88.7 4.3 %all-to-all-start.1 = ((bf16[4,32,3072]{2,1,0:T(8,128)(2,1)}), bf16[4,32,3072]{2,1,0:T(8,128)(2,1)S(1)}, u32[]{:S(2)}, u32[]{:S(2)}) async-start(bf16[4,32,3072]{2,1,0:T(8,128)(2,1)} %bitcast.5), calls=%async_computation.1 | async-start | bytes 1572864 | tf_op jit(solution)/shard_map/all_to_all | solution.py:399
  93.1 0.9 constant_dynamic-slice_fusion.atoms
  94.0 11.1 %all-to-all-done.1.parts = bf16[4,32,3072]{2,1,0:T(8,128)(2,1)S(1)} async-done(((bf16[4,32,3072]{2,1,0:T(8,128)(2,1)}), bf16[4,32,3072]{2,1,0:T(8,128)(2,1)S(1)}, u32[]{:S(2)}, u32[]{:S(2)}) %all-to-all-start.1) | async-done | bytes 786464 | tf_op jit(solution)/shard_map/all_to_all | solution.py:399
  105.1 1.1 finish.1
  (11 shorter events, 0.2 us)
Async XLA Ops:
  0.7 2.8 %copy-start = (bf16[1024,3072]{1,0:T(8,128)(2,1)S(1)}, bf16[1024,3072]{1,0:T(8,128)(2,1)}, u32[]{:S(2)}) copy-start(bf16[1024,3072]{1,0:T(8,128)(2,1)} %source.1) | copy-start | bytes 18874372
  3.5 1.0 copy-start.1
  4.5 0.9 copy-start.3
  10.4 3.7 %collective-permute-start = (f32[3,16,256]{2,1,0:T(8,128)S(1)}, f32[3,16,256]{2,1,0:T(8,128)S(1)}, u32[]{:S(2)}, u32[]{:S(2)}) collective-permute-start(f32[3,16,256]{2,1,0:T(8,128)S(1)} %get-tuple-element.26), channel_id=1, source_target_pairs={{0,1},{1,2},{2,3},{3,4},{4,5},{5,6},{6,7},{8,9},{9,10},{10,11},{11... | collective-permute-start | bytes 147464 | tf_op jit(solution)/shard_map/ppermute | solution.py:317
  12.8 5.2 %collective-permute-start.1 = (f32[3,16,256]{2,1,0:T(8,128)S(1)}, f32[3,16,256]{2,1,0:T(8,128)S(1)}, u32[]{:S(2)}, u32[]{:S(2)}) collective-permute-start(f32[3,16,256]{2,1,0:T(8,128)S(1)} %get-tuple-element.27), channel_id=1, source_target_pairs={{1,0},{2,1},{3,2},{4,3},{5,4},{6,5},{7,6},{9,8},{10,9},{11,10},{12... | collective-permute-start | bytes 147464 | tf_op jit(solution)/shard_map/ppermute | solution.py:317
  18.1 5.5 %collective-permute-start.2 = (f32[3,24,256]{2,1,0:T(8,128)S(1)}, f32[3,24,256]{2,1,0:T(8,128)S(1)}, u32[]{:S(2)}, u32[]{:S(2)}) collective-permute-start(f32[3,24,256]{2,1,0:T(8,128)S(1)} %get-tuple-element.29), channel_id=1, source_target_pairs={{0,8},{8,16},{16,24},{1,9},{9,17},{17,25},{2,10},{10,18},{18,26},{... | collective-permute-start | bytes 221192 | tf_op jit(solution)/shard_map/ppermute | solution.py:317
  21.6 6.2 %collective-permute-start.3 = (f32[3,24,256]{2,1,0:T(8,128)S(1)}, f32[3,24,256]{2,1,0:T(8,128)S(1)}, u32[]{:S(2)}, u32[]{:S(2)}) collective-permute-start(f32[3,24,256]{2,1,0:T(8,128)S(1)} %get-tuple-element.30), channel_id=1, source_target_pairs={{8,0},{16,8},{24,16},{9,1},{17,9},{25,17},{10,2},{18,10},{26,18},{... | collective-permute-start | bytes 221192 | tf_op jit(solution)/shard_map/ppermute | solution.py:317
  32.1 4.6 %collective-permute-start.4 = (f32[3,16,256]{2,1,0:T(8,128)S(1)}, f32[3,16,256]{2,1,0:T(8,128)S(1)}, u32[]{:S(2)}, u32[]{:S(2)}) collective-permute-start(f32[3,16,256]{2,1,0:T(8,128)S(1)} %get-tuple-element.35), channel_id=1, source_target_pairs={{0,1},{1,2},{2,3},{3,4},{4,5},{5,6},{6,7},{8,9},{9,10},{10,11},{11... | collective-permute-start | bytes 147464 | tf_op jit(solution)/shard_map/ppermute | solution.py:317
  35.4 4.0 %collective-permute-start.5 = (f32[3,16,256]{2,1,0:T(8,128)S(1)}, f32[3,16,256]{2,1,0:T(8,128)S(1)}, u32[]{:S(2)}, u32[]{:S(2)}) collective-permute-start(f32[3,16,256]{2,1,0:T(8,128)S(1)} %get-tuple-element.36), channel_id=1, source_target_pairs={{1,0},{2,1},{3,2},{4,3},{5,4},{6,5},{7,6},{9,8},{10,9},{11,10},{12... | collective-permute-start | bytes 147464 | tf_op jit(solution)/shard_map/ppermute | solution.py:317
  39.5 5.5 %collective-permute-start.6 = (f32[3,24,256]{2,1,0:T(8,128)S(1)}, f32[3,24,256]{2,1,0:T(8,128)S(1)}, u32[]{:S(2)}, u32[]{:S(2)}) collective-permute-start(f32[3,24,256]{2,1,0:T(8,128)S(1)} %get-tuple-element.38), channel_id=1, source_target_pairs={{0,8},{8,16},{16,24},{1,9},{9,17},{17,25},{2,10},{10,18},{18,26},{... | collective-permute-start | bytes 221192 | tf_op jit(solution)/shard_map/ppermute | solution.py:317
  43.0 6.2 %collective-permute-start.7 = (f32[3,24,256]{2,1,0:T(8,128)S(1)}, f32[3,24,256]{2,1,0:T(8,128)S(1)}, u32[]{:S(2)}, u32[]{:S(2)}) collective-permute-start(f32[3,24,256]{2,1,0:T(8,128)S(1)} %get-tuple-element.39), channel_id=1, source_target_pairs={{8,0},{16,8},{24,16},{9,1},{17,9},{25,17},{10,2},{18,10},{26,18},{... | collective-permute-start | bytes 221192 | tf_op jit(solution)/shard_map/ppermute | solution.py:317
  49.3 55.9 %copy-start.2 = (f32[32,3072]{1,0:T(8,128)S(1)}, f32[32,3072]{1,0:T(8,128)}, u32[]{:S(2)}) copy-start(f32[32,3072]{1,0:T(8,128)} %momentum.1) | copy-start | bytes 1179652
  54.4 31.3 %all-to-all-start = ((bf16[8,128,128]{2,1,0:T(8,128)(2,1)}), bf16[8,128,128]{2,1,0:T(8,128)(2,1)S(1)}, u32[]{:S(2)}, u32[]{:S(2)}) async-start(bf16[8,128,128]{2,1,0:T(8,128)(2,1)} %get-tuple-element.41), calls=%async_computation | async-start | bytes 524288 | tf_op jit(solution)/shard_map/all_to_all | solution.py:375
  58.2 4.1 %collective-permute-start.8 = (f32[3,16,256]{2,1,0:T(8,128)S(1)}, f32[3,16,256]{2,1,0:T(8,128)S(1)}, u32[]{:S(2)}, u32[]{:S(2)}) collective-permute-start(f32[3,16,256]{2,1,0:T(8,128)S(1)} %get-tuple-element.43), channel_id=1, source_target_pairs={{0,1},{1,2},{2,3},{3,4},{4,5},{5,6},{6,7},{8,9},{9,10},{10,11},{11... | collective-permute-start | bytes 147464 | tf_op jit(solution)/shard_map/ppermute | solution.py:317
  61.0 5.4 %collective-permute-start.9 = (f32[3,16,256]{2,1,0:T(8,128)S(1)}, f32[3,16,256]{2,1,0:T(8,128)S(1)}, u32[]{:S(2)}, u32[]{:S(2)}) collective-permute-start(f32[3,16,256]{2,1,0:T(8,128)S(1)} %get-tuple-element.44), channel_id=1, source_target_pairs={{1,0},{2,1},{3,2},{4,3},{5,4},{6,5},{7,6},{9,8},{10,9},{11,10},{12... | collective-permute-start | bytes 147464 | tf_op jit(solution)/shard_map/ppermute | solution.py:317
  88.7 16.4 %all-to-all-start.1 = ((bf16[4,32,3072]{2,1,0:T(8,128)(2,1)}), bf16[4,32,3072]{2,1,0:T(8,128)(2,1)S(1)}, u32[]{:S(2)}, u32[]{:S(2)}) async-start(bf16[4,32,3072]{2,1,0:T(8,128)(2,1)} %bitcast.5), calls=%async_computation.1 | async-start | bytes 1572864 | tf_op jit(solution)/shard_map/all_to_all | solution.py:399

commit v2 on v1

v2 whole, which is shorter than its diff:
```python
import functools

import jax
import jax.numpy as jnp
from jax import lax
from jax.experimental import pallas as pl
from jax.experimental.pallas import tpu as pltpu
from jax.sharding import Mesh
from jax.sharding import PartitionSpec as P

PATCH_SIDE = 32
STRIDE = 8
SWEEPS = 2
SPAN = PATCH_SIDE // STRIDE
MARGIN = SPAN - 1

THRESHOLD = 0.25
RELAXATION = 0.1
DECAY = 0.9
LEARNING = 0.25
EPSILON = 1e-05

F32 = jnp.float32
BF16 = jnp.bfloat16
VMEM = pl.BlockSpec(memory_space=pltpu.VMEM)
SMEM = pl.BlockSpec(memory_space=pltpu.SMEM)
HBM = pl.BlockSpec(memory_space=pltpu.HBM)
PARAMS = pltpu.CompilerParams(vmem_limit_bytes=24 * 1024 * 1024)


def up_to(value, step):
    return -(-value // step) * step


def shrink(potential):
    return potential - jnp.clip(potential, -THRESHOLD, THRESHOLD)


class Sizes:
    def __init__(self, site_rows, site_cols, atoms, patch_len):
        self.rows, self.cols, self.atoms, self.patch = site_rows, site_cols, atoms, patch_len
        self.cell = patch_len // (SPAN * SPAN)
        self.band = SPAN * self.cell
        self.sites = site_rows * site_cols
        self.tall = site_rows + MARGIN
        self.wide = site_cols + MARGIN
        self.wide_pad = up_to(self.wide, 8)
        self.tall_pad = up_to(self.tall, 16)
        self.lanes = up_to(self.cell, 128)
        self.rim = up_to(MARGIN * self.wide, 16)
        self.packed = up_to(self.tall * self.cols + MARGIN * self.tall_pad, 32)
        self.scale = patch_len ** (-0.5)


class Place:
    def __init__(self, where, rows_n, cols_n):
        self.row, self.col = where[0], where[1]
        self.rows_n, self.cols_n = rows_n, cols_n
        self.owner = self.row * cols_n + self.col

    def pairs(self, axis):
        at, n = (self.row, self.rows_n) if axis == 0 else (self.col, self.cols_n)
        before, after = at > 0, at < n - 1
        odd = at % 2
        return [
            (odd == 0, ((True, after), (False, before))),
            (odd == 1, ((False, before), (True, after))),
        ]


def partners(n):
    even, odd = {}, {}
    for i in range(n):
        even[i] = i ^ 1 if i ^ 1 < n else i
        other = ((i + 1) ^ 1) - 1
        odd[i] = other if 0 <= other < n else (n - 1 if i == 0 and n % 2 == 0 else i)
    if n % 2 == 0:
        odd[n - 1] = 0
    return [sorted(even.items()), sorted(odd.items())]


def reconstruct(z, place, coding, dic, pixels, tall_sum, own, sends, ready=None):
    tall_sum[z.sites :, :] = jnp.zeros((z.tall * z.cols - z.sites, z.band), F32)
    for i in range(SPAN):
        if ready is not None:
            ready(i)
        placed = jnp.dot(
            coding, dic[:, i * z.band : (i + 1) * z.band], preferred_element_type=F32
        )
        start = i * z.cols
        if i == 0:
            tall_sum[0 : z.sites, :] = placed
        else:
            tall_sum[start : start + z.sites, :] += placed
    own[...] = jnp.zeros((z.tall, z.wide_pad, z.lanes), F32)
    own[0 : z.rows, 0 : z.cols, 0 : z.cell] = pixels[...].reshape(z.rows, z.cols, z.cell)
    for j in range(SPAN):
        part = tall_sum[:, j * z.cell : (j + 1) * z.cell].reshape(z.tall, z.cols, z.cell)
        own[:, j : j + z.cols, 0 : z.cell] -= part * z.scale

    @pl.when(place.row == place.rows_n - 1)
    def _():
        own[z.rows :] = jnp.zeros((MARGIN, z.wide_pad, z.lanes), F32)

    @pl.when(place.col == place.cols_n - 1)
    def _():
        own[:, z.cols :] = jnp.zeros((z.tall, z.wide_pad - z.cols, z.lanes), F32)

    for mine, halves in place.pairs(1):

        @pl.when(mine)
        def _(halves=halves):
            for send, (onward, _) in zip(sends, halves):
                first = z.cols if onward else 0
                for c in range(MARGIN):
                    send[c, 0 : z.tall, :] = own[:, first + c, :].astype(BF16)


def add_sides(z, place, whole, received):
    for mine, halves in place.pairs(1):
        for rim, (onward, there) in zip(received, halves):

            @pl.when(mine & there)
            def _(rim=rim, first=z.cols if onward else 0):
                for c in range(MARGIN):
                    whole[:, first + c, :] += rim[c].astype(F32)[0 : z.tall]


def is_equal(a, b):
    return (a == b).astype(F32).astype(BF16)


def cells_of(z, picture, pixels, spread):
    channels, height, width = picture.shape
    flat = picture[...].reshape(channels * height, width)
    high = flat.astype(BF16)
    rest = flat - high.astype(F32)
    middle = rest.astype(BF16)
    low = (rest - middle.astype(F32)).astype(BF16)

    def iota(shape, dim):
        return lax.broadcasted_iota(jnp.int32, shape, dim)

    shape = (channels * height, z.cell)
    line = iota(shape, 0)
    channel, image_row = line // height, line % height
    entry = iota(shape, 1)
    shape = (width, z.cell)
    mine = (iota(shape, 0) % STRIDE == iota(shape, 1) % STRIDE).astype(F32)
    for i in range(z.rows):
        pick = is_equal(
            (channel * STRIDE + image_row - i * STRIDE) * STRIDE + image_row // STRIDE * 65536,
            entry // STRIDE * STRIDE + i * 65536,
        )
        for part, values in enumerate((high, middle, low)):
            moved = lax.dot_general(
                values, pick, (((0,), (0,)), ((), ())), preferred_element_type=F32
            )
            spread[part, i * width : (i + 1) * width, :] = (moved * mine).astype(BF16)
    shape = (z.sites, z.rows * width)
    gather = is_equal(iota(shape, 0), iota(shape, 1) // STRIDE)
    parts = [
        jnp.dot(gather, spread[part], preferred_element_type=F32) for part in range(3)
    ]
    pixels[...] = (parts[0] + parts[1]) + parts[2]


def first_kernel(
    z, grid, where, membrane, picture, source, own, *rest
):
    (*sends, pixels, dic, potential, atoms, tall_sum, spread, drawing, sems) = rest
    place = Place(where, *grid)
    early = [
        pltpu.make_async_copy(picture, drawing, sems.at[SPAN]),
        pltpu.make_async_copy(membrane, potential, sems.at[SPAN + 1]),
    ]
    copies = [
        pltpu.make_async_copy(
            source.at[:, i * z.band : (i + 1) * z.band],
            dic.at[:, i * z.band : (i + 1) * z.band],
            sems.at[i],
        )
        for i in range(SPAN)
    ]
    for copy in early + copies:
        copy.start()
    early[0].wait()
    cells_of(z, drawing, pixels, spread)
    early[1].wait()
    coding = shrink(potential[...]).astype(BF16)
    reconstruct(
        z, place, coding, dic, pixels, tall_sum, own, sends, lambda i: copies[i].wait()
    )
    owned = atoms.shape[0]
    atoms[...] = dic[pl.ds(pl.multiple_of(place.owner * owned, owned), owned), :]


def side_kernel(z, grid, where, own, from_even, from_odd, joined, even, odd, rim):
    place = Place(where, *grid)
    joined[...] = own[...]
    add_sides(z, place, joined, (from_even, from_odd))
    rim[MARGIN * z.wide :, :] = jnp.zeros((z.rim - MARGIN * z.wide, z.lanes), F32)
    for mine, halves in place.pairs(0):

        @pl.when(mine)
        def _(halves=halves):
            for send, (onward, _) in zip((even, odd), halves):
                first = z.rows if onward else 0
                for r in range(MARGIN):
                    start = MARGIN * z.cols + r * MARGIN
                    rim[r * z.cols : (r + 1) * z.cols, :] = joined[first + r, 0 : z.cols, :]
                    rim[start : start + MARGIN, :] = joined[first + r, z.cols : z.wide, :]
                send[...] = rim[...].astype(BF16)


def add_ends(z, place, whole, received, rim):
    for mine, halves in place.pairs(0):
        for block, (onward, there) in zip(received, halves):

            @pl.when(mine & there)
            def _(block=block, first=z.rows if onward else 0):
                rim[...] = block[...].astype(F32)
                for r in range(MARGIN):
                    start = MARGIN * z.cols + r * MARGIN
                    whole[first + r, 0 : z.cols, :] += rim[r * z.cols : (r + 1) * z.cols, :]
                    whole[first + r, z.cols : z.wide, :] += rim[start : start + MARGIN, :]


def windows_of(z, whole, wide_part, first_row, row_stride):
    for j in range(SPAN):
        part = whole[:, j : j + z.cols, 0 : z.cell].astype(BF16)
        for p in range(z.tall):
            wide_part[
                pl.ds(p * row_stride + first_row, z.cols), j * z.cell : (j + 1) * z.cell
            ] = part[p]


def sweep_kernel(
    z, grid, last, groups, where, potential, joined, from_even, from_odd, pixels, dic, *rest
):
    if last:
        new_potential, own, *sends, shared, tall_sum, whole, wide_part, rim = rest
    else:
        new_potential, own, *sends, tall_sum, whole, wide_part, rim = rest
    place = Place(where, *grid)
    whole[...] = joined[...]
    add_ends(z, place, whole, (from_even, from_odd), rim)
    windows_of(z, whole, wide_part, 0, z.cols)
    drive = None
    for i in range(SPAN):
        term = lax.dot_general(
            wide_part[i * z.cols : i * z.cols + z.sites, :],
            dic[:, i * z.band : (i + 1) * z.band],
            (((1,), (1,)), ((), ())),
            preferred_element_type=F32,
        )
        drive = term if drive is None else drive + term
    old = potential[...]
    updated = old + RELAXATION * (drive * z.scale + shrink(old) - old)
    active = shrink(updated)
    coding = active.astype(BF16)
    if last:
        new_potential[...] = active
        rows_n, cores_n, owned = groups
        span = z.atoms // rows_n
        src = lax.broadcasted_iota(jnp.int32, (span, span), 0)
        dst = lax.broadcasted_iota(jnp.int32, (span, span), 1)
        per_core = span // cores_n
        core, rem = dst // per_core, dst % per_core
        wanted = (rem // owned) * (owned * cores_n) + core * owned + rem % owned
        order = is_equal(src, wanted)
        for r in range(rows_n):
            sorted_codes = jnp.dot(
                coding[:, r * span : (r + 1) * span], order, preferred_element_type=F32
            ).astype(BF16)
            for k in range(cores_n):
                shared[r * cores_n + k] = sorted_codes[:, k * per_core : (k + 1) * per_core]
    else:
        new_potential[...] = updated
    reconstruct(z, place, coding, dic, pixels, tall_sum, own, sends)


def pack_kernel(z, grid, where, own, from_even, from_odd, packed, joined, flat):
    joined[...] = own[...]
    add_sides(z, Place(where, *grid), joined, (from_even, from_odd))
    base = z.tall * z.cols
    flat[base:, :] = jnp.zeros((z.packed - base, z.lanes), F32)
    for p in range(z.tall):
        flat[p * z.cols : (p + 1) * z.cols, :] = joined[p, 0 : z.cols, :]
    for c in range(MARGIN):
        start = base + c * z.tall_pad
        flat[start : start + z.tall, :] = joined[:, z.cols + c, :]
    half = z.packed // 2
    packed[0 : z.packed, :] = flat[:, 0:128].astype(BF16)
    tail = z.cell - 128
    ends = jnp.concatenate([flat[0:half, 128 : z.cell], flat[half:, 128 : z.cell]], axis=1)
    packed[z.packed :, 0 : 2 * tail] = ends.astype(BF16)


def learn_kernel(z, groups, where, shared, packed, partial, flat, whole, wide_part, codes):
    rows_n, cores_n, _ = groups
    members = rows_n * cores_n
    stride = members * z.cols
    base = z.tall * z.cols
    half = z.packed // 2
    tail = z.cell - 128
    row = where[0]

    for k in range(cores_n):
        for x in range(rows_n):
            d = (row ^ x) if rows_n & (rows_n - 1) == 0 else (row + x) % rows_n
            block = packed[k, x].astype(F32)
            flat[d, :, 0:128] = block[0 : z.packed]
            flat[d, 0:half, 128 : z.cell] = block[z.packed :, 0:tail]
            flat[d, half:, 128 : z.cell] = block[z.packed :, tail : 2 * tail]
        for r in range(rows_n):
            d = r * cores_n + k
            for source, low, high, at in (
                (r, 0, z.tall, 0),
                (r - 1, z.rows, z.tall, 0),
                (r + 1, 0, MARGIN, z.rows),
            ):
                if not 0 <= source < rows_n:
                    continue
                n = high - low
                main = flat[source, low * z.cols : high * z.cols, :].reshape(n, z.cols, z.lanes)
                side = [
                    flat[source, base + c * z.tall_pad + low : base + c * z.tall_pad + high, :]
                    for c in range(MARGIN)
                ]
                if source == r:
                    whole[at : at + n, 0 : z.cols, :] = main
                    for c in range(MARGIN):
                        whole[at : at + n, z.cols + c, :] = side[c]
                else:
                    whole[at : at + n, 0 : z.cols, :] += main
                    for c in range(MARGIN):
                        whole[at : at + n, z.cols + c, :] += side[c]
            windows_of(z, whole, wide_part, d * z.cols, stride)
            for i in range(z.rows):
                codes[i * stride + d * z.cols : i * stride + (d + 1) * z.cols, :] = shared[
                    d, i * z.cols : (i + 1) * z.cols, :
                ]
    count = z.rows * stride
    across = codes[...].astype(F32).T.astype(BF16)
    for i in range(SPAN):
        term = jnp.dot(
            across, wide_part[i * stride : i * stride + count, :], preferred_element_type=F32
        )
        partial[:, i * z.band : (i + 1) * z.band] = (term * z.scale).astype(BF16)


def finish_kernel(where, parts, momentum, atoms, new_dictionary, new_momentum):
    learning = parts[0].astype(F32)
    for i in range(1, parts.shape[0]):
        learning = learning + parts[i].astype(F32)
    momentum_out = DECAY * momentum[...] + learning
    new_momentum[...] = momentum_out
    weights = atoms[...].astype(F32) + LEARNING * momentum_out
    power = jnp.mean(weights * weights, axis=1, keepdims=True)
    new_dictionary[...] = weights * lax.rsqrt(power + EPSILON)


def kept(x, space=pltpu.VMEM):
    return pltpu.with_memory_space_constraint(x, space)


def call(kernel, outs, inputs, scratch, name, far=0):
    specs = [SMEM] + [HBM] * far + [VMEM] * (len(inputs) - 1 - far)
    where, *others = inputs
    placed = [kept(x, pltpu.HBM) for x in others[:far]] + [kept(x) for x in others[far:]]
    return pl.pallas_call(
        kernel,
        out_shape=outs,
        in_specs=specs,
        out_specs=[VMEM] * len(outs),
        scratch_shapes=scratch,
        compiler_params=PARAMS,
        name=name,
    )(where, *placed)


def shards(picture, membrane, dictionary, momentum):
    site_rows, site_cols, atom_count = membrane.shape
    z = Sizes(site_rows, site_cols, atom_count, dictionary.shape[1])
    rows_n, yx_n, cores_n = (lax.axis_size(a) for a in ("row", "yx", "core"))
    cols_n = yx_n * cores_n
    owned = momentum.shape[0]
    groups = (rows_n, cores_n, owned)
    members = rows_n * cores_n
    grid = (rows_n, cols_n)
    where = jnp.stack([lax.axis_index("row"), lax.axis_index(("yx", "core"))]).astype(jnp.int32)

    def swapped(axis, n, blocks):
        return [lax.ppermute(b, axis, route) for b, route in zip(blocks, partners(n))]

    def sideways(blocks):
        return swapped(("yx", "core"), cols_n, blocks)

    own_v = pltpu.VMEM((z.tall, z.wide_pad, z.lanes), F32)
    side_v = pltpu.VMEM((MARGIN, z.tall_pad, z.lanes), BF16)
    end_v = pltpu.VMEM((z.rim, z.lanes), BF16)
    rim_v = pltpu.VMEM((z.rim, z.lanes), F32)
    tall_v = pltpu.VMEM((z.tall * z.cols, z.band), F32)
    wide_v = pltpu.VMEM((z.tall * z.cols, z.band), BF16)
    site_v = pltpu.VMEM((z.sites, atom_count), F32)
    outs = [own_v, side_v, side_v]

    own, *sides, pixels, dic, potential, atoms = call(
        functools.partial(first_kernel, z, grid),
        outs
        + [
            pltpu.VMEM((z.sites, z.cell), F32),
            pltpu.VMEM(dictionary.shape, BF16),
            site_v,
            pltpu.VMEM(momentum.shape, BF16),
        ],
        (where, membrane.reshape(z.sites, atom_count), picture, dictionary),
        [
            tall_v,
            pltpu.VMEM((3, z.rows * picture.shape[2], z.cell), BF16),
            pltpu.VMEM(picture.shape, F32),
            pltpu.SemaphoreType.DMA((SPAN + 2,)),
        ],
        "first",
        far=3,
    )
    for repeat in range(SWEEPS):
        last = repeat == SWEEPS - 1
        joined, *ends = call(
            functools.partial(side_kernel, z, grid),
            [own_v, end_v, end_v],
            (where, own, *sideways(sides)),
            [rim_v],
            "side",
        )
        ends = swapped("row", rows_n, ends)
        final = [
            jax.ShapeDtypeStruct((z.sites, atom_count), F32),
            *outs,
            pltpu.VMEM((members, z.sites, atom_count // members), BF16),
        ]
        potential, own, *rest = call(
            functools.partial(sweep_kernel, z, grid, last, groups),
            final if last else [site_v] + outs,
            (where, potential, joined, *ends, pixels, dic),
            [tall_v, own_v, wide_v, rim_v],
            "sweep",
        )
        sides = rest[:2]
    final_codes = potential.reshape(membrane.shape)
    shared = lax.all_to_all(rest[2], ("row", "core"), 0, 0, tiled=True)
    (packed,) = call(
        functools.partial(pack_kernel, z, grid),
        [pltpu.VMEM((z.packed * 3 // 2, 128), BF16)],
        (where, own, *sideways(sides)),
        [own_v, pltpu.VMEM((z.packed, z.lanes), F32)],
        "pack",
    )
    blocks = [packed]
    for x in range(1, rows_n):
        power = rows_n & (rows_n - 1) == 0
        route = [(i ^ x if power else (i + x) % rows_n, i) for i in range(rows_n)]
        blocks.append(lax.ppermute(packed, "row", route))
    blocks = lax.all_gather(jnp.stack(blocks), "core", axis=0, tiled=False)
    (partial,) = call(
        functools.partial(learn_kernel, z, groups),
        [pltpu.VMEM((atom_count // members, z.patch), BF16)],
        (where, shared, blocks),
        [
            pltpu.VMEM((rows_n, z.packed, z.lanes), F32),
            own_v,
            pltpu.VMEM((z.tall * members * z.cols, z.band), BF16),
            pltpu.VMEM((members * z.sites, atom_count // members), BF16),
        ],
        "learn",
    )
    parts = lax.all_to_all(partial.reshape(yx_n, owned, z.patch), "yx", 0, 0, tiled=True)
    new_dictionary, new_momentum = call(
        finish_kernel,
        [jax.ShapeDtypeStruct(momentum.shape, F32)] * 2,
        (where, parts, momentum, atoms),
        [],
        "finish",
    )
    return (final_codes, new_dictionary, new_momentum)


def solution(mesh):
    rows_n, cols_n = (mesh.shape["row"], mesh.shape["col"])
    cores_n = 2 if cols_n % 2 == 0 else 1
    split = Mesh(
        mesh.devices.reshape(rows_n, cols_n // cores_n, cores_n), ("row", "yx", "core")
    )
    col = ("yx", "core")
    return jax.shard_map(
        shards,
        mesh=split,
        in_specs=(P(None, "row", col), P("row", col, None), P(), P(("row",) + col, None)),
        out_specs=(P("row", col, None), P(("row",) + col, None), P(("row",) + col, None)),
        check_vma=False,
    )
```

time: 107 us -> 82.6 us (0.77)
  waiting for transfers between devices: 31.7 us -> 20.9 us
  starting transfers between devices: 30.1 us -> 22.5 us
  local copies, waits for them, and re-layouts: 5.66 us -> 0.01 us
  Pallas kernels: 18.7 us -> 21.3 us
  blocking collectives: 19.2 us -> 16.8 us
    all_gather x1, blocking collectives: 19.2 us -> 2.48 us  [shards(): blocks = lax.all_gather(jnp.stack(blocks), 'core', axis=0, tiled=False)]
    all_to_all x0 -> x1, blocking collectives: none -> 14.3 us  [shards(): lax.all_to_all(partial.reshape(yx_n, owned, z.patch), 'yx', 0, 0, tiled=T...]
    all_to_all x2 -> x1, waiting for transfers between devices: 11.1 us -> 0.01 us  [shards(): shared = lax.all_to_all(rest[2], ('row', 'core'), 0, 0, tiled=True)]
    unnamed x8 -> x2, local copies, waits for them, and re-layouts: 4.72 us -> 0.01 us
    all_to_all x2 -> x1, starting transfers between devices: 8.15 us -> 3.74 us  [shards(): shared = lax.all_to_all(rest[2], ('row', 'core'), 0, 0, tiled=True)]
    ppermute x10 -> x13, starting transfers between devices: 21.9 us -> 18.7 us  [the longest x10 14.3 us: swapped(): lax.ppermute(b, axis, route)]
    pallas_call x8, Pallas kernels: 18.7 us -> 21.3 us  [call(): pl.pallas_call(kernel, out_shape=outs, in_specs=specs, out_specs=[VMEM] *...]
    ppermute x10 -> x13, waiting for transfers between devices: 20.6 us -> 20.9 us  [the longest x10 13.6 us: swapped(): lax.ppermute(b, axis, route)]
  transfers between devices with their start and end apart: 12 -> 14, of which waited for: 8 -> 9; matrix products, arithmetic and copies ran while one was open for 1% -> 0% of each run, Pallas kernels for 0% -> 1%
where the time goes in v2:
time: 82.6 us; the launch traced here: 82.3 us
  starting transfers between devices  22.5 us (27%)
  Pallas kernels  21.3 us (26%)
  waiting for transfers between devices  20.9 us (25%)
  blocking collectives  16.8 us (20%)
    pallas_call x8, Pallas kernels, call(): pl.pallas_call(kernel, out_shape=outs, in_specs=specs, out_specs=[VMEM] *...  21.3 us
    all_to_all x1, blocking collectives, shards(): lax.all_to_all(partial.reshape(yx_n, owned, z.patch), 'yx', 0, 0, tiled=T...  14.3 us
    ppermute x10, starting transfers between devices, swapped(): lax.ppermute(b, axis, route)  14.3 us
    ppermute x10, waiting for transfers between devices, swapped(): lax.ppermute(b, axis, route)  13.6 us
    ppermute x3, waiting for transfers between devices, shards(): blocks.append(lax.ppermute(packed, 'row', route))  7.29 us
    ppermute x3, starting transfers between devices, shards(): blocks.append(lax.ppermute(packed, 'row', route))  4.44 us
    all_to_all x1, starting transfers between devices, shards(): shared = lax.all_to_all(rest[2], ('row', 'core'), 0, 0, tiled=True)  3.74 us
    all_gather x1, blocking collectives, shards(): blocks = lax.all_gather(jnp.stack(blocks), 'core', axis=0, tiled=False)  2.48 us
  transfers between devices with their start and end apart: 14, of which 9 were waited for; matrix products, arithmetic and copies ran while one was open for 0% of the time, Pallas kernels for 1%

profile of v2, /device:TPU:0, one launch (start us, length us, event | category | flops | bytes accessed | tf_op | source)
XLA Modules:
  0.0 82.3 jit_solution(3697962314759060010)
XLA Ops:
  0.6 0.1 pad_add_fusion.where
  0.7 5.2 %first.1 = (f32[11,24,256]{2,1,0:T(8,128)S(1)}, bf16[3,16,256]{2,1,0:T(8,128)(2,1)S(1)}, bf16[3,16,256]{2,1,0:T(8,128)(2,1)S(1)}, f32[128,192]{1,0:T(8,128)S(1)}...) custom-call(s32[2]{0:T(128)S(1)} %pad_add_fusion.where, ...), custom_call_target="tpu_custom_call" | custom-call | tf_op jit(solution)/shard_map/first/pallas_call | solution.py:372
  6.0 0.6 collective-permute-start
  6.5 3.5 %collective-permute-start.1 = (bf16[3,16,256]{2,1,0:T(8,128)(2,1)S(1)}, bf16[3,16,256]{2,1,0:T(8,128)(2,1)S(1)}, u32[]{:S(2)}, u32[]{:S(2)}) collective-permute-start(bf16[3,16,256]{2,1,0:T(8,128)(2,1)S(1)} %get-tuple-element.30), channel_id=1, source_target_pairs={{0,7},{1,2},{2,1},{3,4},{4,3},{5,6},{6,5},{7,0},{8,15},{9,10},{10,... | collective-permute-start | bytes 73736 | tf_op jit(solution)/shard_map/ppermute | solution.py:395
  10.1 1.5 %collective-permute-done.1.from_odd = bf16[3,16,256]{2,1,0:T(8,128)(2,1)S(1)} collective-permute-done((bf16[3,16,256]{2,1,0:T(8,128)(2,1)S(1)}, bf16[3,16,256]{2,1,0:T(8,128)(2,1)S(1)}, u32[]{:S(2)}, u32[]{:S(2)}) %collective-permute-start.1) | collective-permute-done | bytes 24608 | tf_op jit(solution)/shard_map/ppermute | solution.py:395
  11.6 0.6 side.2
  12.2 1.8 %collective-permute-start.2 = (bf16[64,256]{1,0:T(8,128)(2,1)S(1)}, bf16[64,256]{1,0:T(8,128)(2,1)S(1)}, u32[]{:S(2)}, u32[]{:S(2)}) collective-permute-start(bf16[64,256]{1,0:T(8,128)(2,1)S(1)} %get-tuple-element.32), channel_id=1, source_target_pairs={{0,8},{8,0},{16,24},{24,16},{1,9},{9,1},{17,25},{25,17},{2,10},{10... | collective-permute-start | bytes 98312 | tf_op jit(solution)/shard_map/ppermute | solution.py:395
  14.0 2.5 %collective-permute-start.3 = (bf16[64,256]{1,0:T(8,128)(2,1)S(1)}, bf16[64,256]{1,0:T(8,128)(2,1)S(1)}, u32[]{:S(2)}, u32[]{:S(2)}) collective-permute-start(bf16[64,256]{1,0:T(8,128)(2,1)S(1)} %get-tuple-element.33), channel_id=1, source_target_pairs={{0,24},{8,16},{16,8},{24,0},{1,25},{9,17},{17,9},{25,1},{2,26},{10... | collective-permute-start | bytes 98312 | tf_op jit(solution)/shard_map/ppermute | solution.py:395
  16.5 3.2 %collective-permute-done.3.from_odd = bf16[64,256]{1,0:T(8,128)(2,1)S(1)} collective-permute-done((bf16[64,256]{1,0:T(8,128)(2,1)S(1)}, bf16[64,256]{1,0:T(8,128)(2,1)S(1)}, u32[]{:S(2)}, u32[]{:S(2)}) %collective-permute-start.3) | collective-permute-done | bytes 32800 | tf_op jit(solution)/shard_map/ppermute | solution.py:395
  19.7 4.3 %sweep.2 = (f32[128,1024]{1,0:T(8,128)S(1)}, f32[11,24,256]{2,1,0:T(8,128)S(1)}, bf16[3,16,256]{2,1,0:T(8,128)(2,1)S(1)}, bf16[3,16,256]{2,1,0:T(8,128)(2,1)S(1)}) custom-call(s32[2]{0:T(128)S(1)} %pad_add_fusion.where, f32[128,1024]{1,0:T(8,128)S(1)} %get-tuple-element.27.potential, f32[11,24,256]{2,1,0:T(8,128)S(1)} %get-tuple-element.31.joined, ...), custom_call_target="tpu_custom_call" | custom-call | tf_op jit(solution)/shard_map/sweep/pallas_call | solution.py:372
  24.1 0.1 collective-permute-start.4
  24.2 2.0 %collective-permute-start.5 = (bf16[3,16,256]{2,1,0:T(8,128)(2,1)S(1)}, bf16[3,16,256]{2,1,0:T(8,128)(2,1)S(1)}, u32[]{:S(2)}, u32[]{:S(2)}) collective-permute-start(bf16[3,16,256]{2,1,0:T(8,128)(2,1)S(1)} %get-tuple-element.39), channel_id=1, source_target_pairs={{0,7},{1,2},{2,1},{3,4},{4,3},{5,6},{6,5},{7,0},{8,15},{9,10},{10,... | collective-permute-start | bytes 73736 | tf_op jit(solution)/shard_map/ppermute | solution.py:395
  26.1 2.3 %collective-permute-done.5.from_odd = bf16[3,16,256]{2,1,0:T(8,128)(2,1)S(1)} collective-permute-done((bf16[3,16,256]{2,1,0:T(8,128)(2,1)S(1)}, bf16[3,16,256]{2,1,0:T(8,128)(2,1)S(1)}, u32[]{:S(2)}, u32[]{:S(2)}) %collective-permute-start.5) | collective-permute-done | bytes 24608 | tf_op jit(solution)/shard_map/ppermute | solution.py:395
  28.4 0.6 side.3
  29.1 2.5 %collective-permute-start.7 = (bf16[64,256]{1,0:T(8,128)(2,1)S(1)}, bf16[64,256]{1,0:T(8,128)(2,1)S(1)}, u32[]{:S(2)}, u32[]{:S(2)}) collective-permute-start(bf16[64,256]{1,0:T(8,128)(2,1)S(1)} %get-tuple-element.42), channel_id=1, source_target_pairs={{0,24},{8,16},{16,8},{24,0},{1,25},{9,17},{17,9},{25,1},{2,26},{10... | collective-permute-start | bytes 98312 | tf_op jit(solution)/shard_map/ppermute | solution.py:395
  31.6 1.4 %collective-permute-done.6.from_even = bf16[64,256]{1,0:T(8,128)(2,1)S(1)} collective-permute-done((bf16[64,256]{1,0:T(8,128)(2,1)S(1)}, bf16[64,256]{1,0:T(8,128)(2,1)S(1)}, u32[]{:S(2)}, u32[]{:S(2)}) %collective-permute-start.6) | collective-permute-done | bytes 32800 | tf_op jit(solution)/shard_map/ppermute | solution.py:395
  33.0 1.9 %collective-permute-done.7.from_odd = bf16[64,256]{1,0:T(8,128)(2,1)S(1)} collective-permute-done((bf16[64,256]{1,0:T(8,128)(2,1)S(1)}, bf16[64,256]{1,0:T(8,128)(2,1)S(1)}, u32[]{:S(2)}, u32[]{:S(2)}) %collective-permute-start.7) | collective-permute-done | bytes 32800 | tf_op jit(solution)/shard_map/ppermute | solution.py:395
  34.9 5.3 %sweep.3 = (f32[128,1024]{1,0:T(8,128)}, f32[11,24,256]{2,1,0:T(8,128)S(1)}, bf16[3,16,256]{2,1,0:T(8,128)(2,1)S(1)}, bf16[3,16,256]{2,1,0:T(8,128)(2,1)S(1)}, bf16[8,128,128]{2,1,0:T(8,128)(2,1)}) custom-call(s32[2]{0:T(128)S(1)} %pad_add_fusion.where, f32[128,1024]{1,0:T(8,128)S(1)} %get-tuple-element.36.potential, ...), custom_call_target="tpu_custom_call" | custom-call | tf_op jit(solution)/shard_map/sweep/pallas_call | solution.py:372
  40.1 3.7 %all-to-all-start = ((bf16[8,128,128]{2,1,0:T(8,128)(2,1)}), bf16[8,128,128]{2,1,0:T(8,128)(2,1)S(1)}, u32[]{:S(2)}, u32[]{:S(2)}) async-start(bf16[8,128,128]{2,1,0:T(8,128)(2,1)} %get-tuple-element.44), calls=%async_computation | async-start | bytes 524288 | tf_op jit(solution)/shard_map/all_to_all | solution.py:452
  43.9 0.5 collective-permute-start.8
  44.4 0.8 collective-permute-start.9
  45.1 0.2 collective-permute-done.8.from_even
  45.3 3.2 %collective-permute-done.9.from_odd = bf16[3,16,256]{2,1,0:T(8,128)(2,1)S(1)} collective-permute-done((bf16[3,16,256]{2,1,0:T(8,128)(2,1)S(1)}, bf16[3,16,256]{2,1,0:T(8,128)(2,1)S(1)}, u32[]{:S(2)}, u32[]{:S(2)}) %collective-permute-start.9) | collective-permute-done | bytes 24608 | tf_op jit(solution)/shard_map/ppermute | solution.py:395
  48.5 0.7 pack.1
  49.2 3.5 %collective-permute-start.12 = (bf16[336,128]{1,0:T(8,128)(2,1)S(1)}, bf16[336,128]{1,0:T(8,128)(2,1)S(1)}, u32[]{:S(2)}, u32[]{:S(2)}) collective-permute-start(bf16[336,128]{1,0:T(8,128)(2,1)S(1)} %pack.1), channel_id=1, source_target_pairs={{24,0},{16,8},{8,16},{0,24},{25,1},{17,9},{9,17},{1,25},{26,2},{18... | collective-permute-start | bytes 258056 | tf_op jit(solution)/shard_map/ppermute | solution.py:464
  52.7 1.0 %collective-permute-start.10 = (bf16[336,128]{1,0:T(8,128)(2,1)S(1)}, bf16[336,128]{1,0:T(8,128)(2,1)S(1)}, u32[]{:S(2)}, u32[]{:S(2)}) collective-permute-start(bf16[336,128]{1,0:T(8,128)(2,1)S(1)} %pack.1), channel_id=1, source_target_pairs={{8,0},{0,8},{24,16},{16,24},{9,1},{1,9},{25,17},{17,25},{10,2},{2,... | collective-permute-start | bytes 258056 | tf_op jit(solution)/shard_map/ppermute | solution.py:464
  53.7 2.6 %collective-permute-done.12 = bf16[336,128]{1,0:T(8,128)(2,1)S(1)} collective-permute-done((bf16[336,128]{1,0:T(8,128)(2,1)S(1)}, bf16[336,128]{1,0:T(8,128)(2,1)S(1)}, u32[]{:S(2)}, u32[]{:S(2)}) %collective-permute-start.12) | collective-permute-done | bytes 86048 | tf_op jit(solution)/shard_map/ppermute | solution.py:464
  56.3 4.7 %collective-permute-done.11 = bf16[336,128]{1,0:T(8,128)(2,1)S(1)} collective-permute-done((bf16[336,128]{1,0:T(8,128)(2,1)S(1)}, bf16[336,128]{1,0:T(8,128)(2,1)S(1)}, u32[]{:S(2)}, u32[]{:S(2)}) %collective-permute-start.11) | collective-permute-done | bytes 86048 | tf_op jit(solution)/shard_map/ppermute | solution.py:464
  61.0 2.5 %all-gather = bf16[8,336,128]{2,1,0:T(8,128)(2,1)S(1)} all-gather(bf16[4,336,128]{2,1,0:T(8,128)(2,1)S(1)} %pad_maximum_fusion), channel_id=2, replica_groups=mesh['row'=4,'yx'=4,'core'=2] {'core'}, dimensions={0}, use_global_device_ids=true | all-gather | bytes 1032192 | tf_op jit(solution)/shard_map/all_gather | solution.py:465
  63.5 2.9 %learn.1 = bf16[128,3072]{1,0:T(8,128)(2,1)S(1)} custom-call(s32[2]{0:T(128)S(1)} %pad_add_fusion.where, bf16[8,128,128]{2,1,0:T(8,128)(2,1)S(1)} %all-to-all-done.shared, bf16[2,4,336,128]{3,2,1,0:T(8,128)(2,1)S(1)} %bitcast.11), custom_call_target="tpu_custom_call" | custom-call | tf_op jit(solution)/shard_map/learn/pallas_call | solution.py:372
  66.4 14.3 %all_to_all.10.parts = bf16[4,32,3072]{2,1,0:T(8,128)(2,1)S(1)} all-to-all(bf16[4,32,3072]{2,1,0:T(8,128)(2,1)S(1)} %bitcast.10), channel_id=1, replica_groups=mesh['row'=4,'yx'=4,'core'=2] {'yx'}, dimensions={0} | all-to-all | bytes 1572864 | tf_op jit(solution)/shard_map/all_to_all | solution.py:478
  80.7 1.6 %finish.1 = (f32[32,3072]{1,0:T(8,128)}, f32[32,3072]{1,0:T(8,128)}) custom-call(s32[2]{0:T(128)S(1)} %pad_add_fusion.where, bf16[4,32,3072]{2,1,0:T(8,128)(2,1)S(1)} %all_to_all.10.parts, f32[32,3072]{1,0:T(8,128)S(1)} %copy-done, bf16[32,3072]{1,0:T(8,128)(2,1)S(1)} %get-tuple-element.48.atoms), custom_call_target="tpu_custom_call" | custom-call | tf_op jit(solution)/shard_map/finish/pallas_call | solution.py:372
  (10 shorter events, 0.1 us)
Async XLA Ops:
  6.0 4.1 %collective-permute-start = (bf16[3,16,256]{2,1,0:T(8,128)(2,1)S(1)}, bf16[3,16,256]{2,1,0:T(8,128)(2,1)S(1)}, u32[]{:S(2)}, u32[]{:S(2)}) collective-permute-start(bf16[3,16,256]{2,1,0:T(8,128)(2,1)S(1)} %get-tuple-element.29), channel_id=1, source_target_pairs={{0,1},{1,0},{2,3},{3,2},{4,5},{5,4},{6,7},{7,6},{8,9},{9,8},{10,11... | collective-permute-start | bytes 73736 | tf_op jit(solution)/shard_map/ppermute | solution.py:395
  6.5 5.1 %collective-permute-start.1 = (bf16[3,16,256]{2,1,0:T(8,128)(2,1)S(1)}, bf16[3,16,256]{2,1,0:T(8,128)(2,1)S(1)}, u32[]{:S(2)}, u32[]{:S(2)}) collective-permute-start(bf16[3,16,256]{2,1,0:T(8,128)(2,1)S(1)} %get-tuple-element.30), channel_id=1, source_target_pairs={{0,7},{1,2},{2,1},{3,4},{4,3},{5,6},{6,5},{7,0},{8,15},{9,10},{10,... | collective-permute-start | bytes 73736 | tf_op jit(solution)/shard_map/ppermute | solution.py:395
  12.2 4.3 %collective-permute-start.2 = (bf16[64,256]{1,0:T(8,128)(2,1)S(1)}, bf16[64,256]{1,0:T(8,128)(2,1)S(1)}, u32[]{:S(2)}, u32[]{:S(2)}) collective-permute-start(bf16[64,256]{1,0:T(8,128)(2,1)S(1)} %get-tuple-element.32), channel_id=1, source_target_pairs={{0,8},{8,0},{16,24},{24,16},{1,9},{9,1},{17,25},{25,17},{2,10},{10... | collective-permute-start | bytes 98312 | tf_op jit(solution)/shard_map/ppermute | solution.py:395
  14.0 5.7 %collective-permute-start.3 = (bf16[64,256]{1,0:T(8,128)(2,1)S(1)}, bf16[64,256]{1,0:T(8,128)(2,1)S(1)}, u32[]{:S(2)}, u32[]{:S(2)}) collective-permute-start(bf16[64,256]{1,0:T(8,128)(2,1)S(1)} %get-tuple-element.33), channel_id=1, source_target_pairs={{0,24},{8,16},{16,8},{24,0},{1,25},{9,17},{17,9},{25,1},{2,26},{10... | collective-permute-start | bytes 98312 | tf_op jit(solution)/shard_map/ppermute | solution.py:395
  24.1 2.0 %collective-permute-start.4 = (bf16[3,16,256]{2,1,0:T(8,128)(2,1)S(1)}, bf16[3,16,256]{2,1,0:T(8,128)(2,1)S(1)}, u32[]{:S(2)}, u32[]{:S(2)}) collective-permute-start(bf16[3,16,256]{2,1,0:T(8,128)(2,1)S(1)} %get-tuple-element.38), channel_id=1, source_target_pairs={{0,1},{1,0},{2,3},{3,2},{4,5},{5,4},{6,7},{7,6},{8,9},{9,8},{10,11... | collective-permute-start | bytes 73736 | tf_op jit(solution)/shard_map/ppermute | solution.py:395
  24.2 4.2 %collective-permute-start.5 = (bf16[3,16,256]{2,1,0:T(8,128)(2,1)S(1)}, bf16[3,16,256]{2,1,0:T(8,128)(2,1)S(1)}, u32[]{:S(2)}, u32[]{:S(2)}) collective-permute-start(bf16[3,16,256]{2,1,0:T(8,128)(2,1)S(1)} %get-tuple-element.39), channel_id=1, source_target_pairs={{0,7},{1,2},{2,1},{3,4},{4,3},{5,6},{6,5},{7,0},{8,15},{9,10},{10,... | collective-permute-start | bytes 73736 | tf_op jit(solution)/shard_map/ppermute | solution.py:395
  29.0 4.0 %collective-permute-start.6 = (bf16[64,256]{1,0:T(8,128)(2,1)S(1)}, bf16[64,256]{1,0:T(8,128)(2,1)S(1)}, u32[]{:S(2)}, u32[]{:S(2)}) collective-permute-start(bf16[64,256]{1,0:T(8,128)(2,1)S(1)} %get-tuple-element.41), channel_id=1, source_target_pairs={{0,8},{8,0},{16,24},{24,16},{1,9},{9,1},{17,25},{25,17},{2,10},{10... | collective-permute-start | bytes 98312 | tf_op jit(solution)/shard_map/ppermute | solution.py:395
  29.1 5.8 %collective-permute-start.7 = (bf16[64,256]{1,0:T(8,128)(2,1)S(1)}, bf16[64,256]{1,0:T(8,128)(2,1)S(1)}, u32[]{:S(2)}, u32[]{:S(2)}) collective-permute-start(bf16[64,256]{1,0:T(8,128)(2,1)S(1)} %get-tuple-element.42), channel_id=1, source_target_pairs={{0,24},{8,16},{16,8},{24,0},{1,25},{9,17},{17,9},{25,1},{2,26},{10... | collective-permute-start | bytes 98312 | tf_op jit(solution)/shard_map/ppermute | solution.py:395
  34.9 45.8 %copy-start = (f32[32,3072]{1,0:T(8,128)S(1)}, f32[32,3072]{1,0:T(8,128)}, u32[]{:S(2)}) copy-start(f32[32,3072]{1,0:T(8,128)} %momentum.1) | copy-start | bytes 1179652
  40.1 23.4 %all-to-all-start = ((bf16[8,128,128]{2,1,0:T(8,128)(2,1)}), bf16[8,128,128]{2,1,0:T(8,128)(2,1)S(1)}, u32[]{:S(2)}, u32[]{:S(2)}) async-start(bf16[8,128,128]{2,1,0:T(8,128)(2,1)} %get-tuple-element.44), calls=%async_computation | async-start | bytes 524288 | tf_op jit(solution)/shard_map/all_to_all | solution.py:452
  43.9 1.4 %collective-permute-start.8 = (bf16[3,16,256]{2,1,0:T(8,128)(2,1)S(1)}, bf16[3,16,256]{2,1,0:T(8,128)(2,1)S(1)}, u32[]{:S(2)}, u32[]{:S(2)}) collective-permute-start(bf16[3,16,256]{2,1,0:T(8,128)(2,1)S(1)} %get-tuple-element.46), channel_id=1, source_target_pairs={{0,1},{1,0},{2,3},{3,2},{4,5},{5,4},{6,7},{7,6},{8,9},{9,8},{10,11... | collective-permute-start | bytes 73736 | tf_op jit(solution)/shard_map/ppermute | solution.py:395
  44.4 4.2 %collective-permute-start.9 = (bf16[3,16,256]{2,1,0:T(8,128)(2,1)S(1)}, bf16[3,16,256]{2,1,0:T(8,128)(2,1)S(1)}, u32[]{:S(2)}, u32[]{:S(2)}) collective-permute-start(bf16[3,16,256]{2,1,0:T(8,128)(2,1)S(1)} %get-tuple-element.47), channel_id=1, source_target_pairs={{0,7},{1,2},{2,1},{3,4},{4,3},{5,6},{6,5},{7,0},{8,15},{9,10},{10,... | collective-permute-start | bytes 73736 | tf_op jit(solution)/shard_map/ppermute | solution.py:395
  49.2 7.1 %collective-permute-start.12 = (bf16[336,128]{1,0:T(8,128)(2,1)S(1)}, bf16[336,128]{1,0:T(8,128)(2,1)S(1)}, u32[]{:S(2)}, u32[]{:S(2)}) collective-permute-start(bf16[336,128]{1,0:T(8,128)(2,1)S(1)} %pack.1), channel_id=1, source_target_pairs={{24,0},{16,8},{8,16},{0,24},{25,1},{17,9},{9,17},{1,25},{26,2},{18... | collective-permute-start | bytes 258056 | tf_op jit(solution)/shard_map/ppermute | solution.py:464
  52.7 8.2 %collective-permute-start.11 = (bf16[336,128]{1,0:T(8,128)(2,1)S(1)}, bf16[336,128]{1,0:T(8,128)(2,1)S(1)}, u32[]{:S(2)}, u32[]{:S(2)}) collective-permute-start(bf16[336,128]{1,0:T(8,128)(2,1)S(1)} %pack.1), channel_id=1, source_target_pairs={{16,0},{24,8},{0,16},{8,24},{17,1},{25,9},{1,17},{9,25},{18,2},{26... | collective-permute-start | bytes 258056 | tf_op jit(solution)/shard_map/ppermute | solution.py:464
  52.7 8.2 %collective-permute-start.10 = (bf16[336,128]{1,0:T(8,128)(2,1)S(1)}, bf16[336,128]{1,0:T(8,128)(2,1)S(1)}, u32[]{:S(2)}, u32[]{:S(2)}) collective-permute-start(bf16[336,128]{1,0:T(8,128)(2,1)S(1)} %pack.1), channel_id=1, source_target_pairs={{8,0},{0,8},{24,16},{16,24},{9,1},{1,9},{25,17},{17,25},{10,2},{2,... | collective-permute-start | bytes 258056 | tf_op jit(solution)/shard_map/ppermute | solution.py:464

commit v3 on v2

--- a/solution.py
+++ b/solution.py
@@ -79,7 +79,7 @@
     return [sorted(even.items()), sorted(odd.items())]
 
 
-def reconstruct(z, place, coding, dic, pixels, tall_sum, own, sends, ready=None):
+def reconstruct(z, place, coding, dic, pixels, tall_sum, own, ready=None):
     tall_sum[z.sites :, :] = jnp.zeros((z.tall * z.cols - z.sites, z.band), F32)
     for i in range(SPAN):
         if ready is not None:
@@ -106,6 +106,8 @@
     def _():
         own[:, z.cols :] = jnp.zeros((z.tall, z.wide_pad - z.cols, z.lanes), F32)
 
+
+def send_sides(z, place, own, sends):
     for mine, halves in place.pairs(1):
 
         @pl.when(mine)
@@ -116,6 +118,31 @@
                     send[c, 0 : z.tall, :] = own[:, first + c, :].astype(BF16)
 
 
+def send_all(z, place, own, flat, packed, outer):
+    base = z.tall * z.cols
+    flat[base:, :] = jnp.zeros((z.packed - base, z.lanes), F32)
+    for p in range(z.tall):
+        flat[p * z.cols : (p + 1) * z.cols, :] = own[p, 0 : z.cols, :]
+    for c in range(MARGIN):
+        start = base + c * z.tall_pad
+        flat[start : start + z.tall, :] = own[:, z.cols + c, :]
+    half = z.packed // 2
+    packed[0 : z.packed, :] = flat[:, 0:128].astype(BF16)
+    tail = z.cell - 128
+    ends = jnp.concatenate([flat[0:half, 128 : z.cell], flat[half:, 128 : z.cell]], axis=1)
+    packed[z.packed :, 0 : 2 * tail] = ends.astype(BF16)
+    for odd, first in ((0, 0), (1, z.cols)):
+
+        @pl.when(place.col % 2 == odd)
+        def _(first=first):
+            for c in range(MARGIN):
+                start = 2 * c * z.tall_pad
+                line = own[:, first + c, :].astype(BF16)
+                outer[start : start + z.tall, :] = line[:, 0:128]
+                start += z.tall_pad
+                outer[start : start + z.tall, 0:tail] = line[:, 128 : z.cell]
+
+
 def add_sides(z, place, whole, received):
     for mine, halves in place.pairs(1):
         for rim, (onward, there) in zip(received, halves):
@@ -132,37 +159,34 @@
 
 def cells_of(z, picture, pixels, spread):
     channels, height, width = picture.shape
-    flat = picture[...].reshape(channels * height, width)
-    high = flat.astype(BF16)
-    rest = flat - high.astype(F32)
+    turned = picture[...].reshape(channels * height, width).T
+    high = turned.astype(BF16)
+    rest = turned - high.astype(F32)
     middle = rest.astype(BF16)
-    low = (rest - middle.astype(F32)).astype(BF16)
+    spread[0:width, :] = high
+    spread[width : 2 * width, :] = middle
+    spread[2 * width :, :] = (rest - middle.astype(F32)).astype(BF16)
 
     def iota(shape, dim):
         return lax.broadcasted_iota(jnp.int32, shape, dim)
 
     shape = (channels * height, z.cell)
-    line = iota(shape, 0)
+    line, entry = iota(shape, 0), iota(shape, 1)
     channel, image_row = line // height, line % height
-    entry = iota(shape, 1)
+    away = (
+        (channel * STRIDE + image_row % STRIDE) * STRIDE
+        + image_row // STRIDE * z.cell
+        - entry // STRIDE * STRIDE
+    )
     shape = (width, z.cell)
     mine = (iota(shape, 0) % STRIDE == iota(shape, 1) % STRIDE).astype(F32)
     for i in range(z.rows):
-        pick = is_equal(
-            (channel * STRIDE + image_row - i * STRIDE) * STRIDE + image_row // STRIDE * 65536,
-            entry // STRIDE * STRIDE + i * 65536,
-        )
-        for part, values in enumerate((high, middle, low)):
-            moved = lax.dot_general(
-                values, pick, (((0,), (0,)), ((), ())), preferred_element_type=F32
-            )
-            spread[part, i * width : (i + 1) * width, :] = (moved * mine).astype(BF16)
-    shape = (z.sites, z.rows * width)
-    gather = is_equal(iota(shape, 0), iota(shape, 1) // STRIDE)
-    parts = [
-        jnp.dot(gather, spread[part], preferred_element_type=F32) for part in range(3)
-    ]
-    pixels[...] = (parts[0] + parts[1]) + parts[2]
+        moved = jnp.dot(
+            spread[...], is_equal(away, i * z.cell), preferred_element_type=F32
+        )
+        whole = (moved[0:width] + moved[width : 2 * width]) + moved[2 * width :]
+        whole = (whole * mine).reshape(z.cols, STRIDE, z.cell)
+        pixels[i * z.cols : (i + 1) * z.cols, :] = jnp.sum(whole, axis=1)
 
 
 def first_kernel(
@@ -188,9 +212,8 @@
     cells_of(z, drawing, pixels, spread)
     early[1].wait()
     coding = shrink(potential[...]).astype(BF16)
-    reconstruct(
-        z, place, coding, dic, pixels, tall_sum, own, sends, lambda i: copies[i].wait()
-    )
+    reconstruct(z, place, coding, dic, pixels, tall_sum, own, lambda i: copies[i].wait())
+    send_sides(z, place, own, sends)
     owned = atoms.shape[0]
     atoms[...] = dic[pl.ds(pl.multiple_of(place.owner * owned, owned), owned), :]
 
@@ -239,7 +262,7 @@
     z, grid, last, groups, where, potential, joined, from_even, from_odd, pixels, dic, *rest
 ):
     if last:
-        new_potential, own, *sends, shared, tall_sum, whole, wide_part, rim = rest
+        new_potential, packed, outer, shared, tall_sum, whole, wide_part, rim, own, flat = rest
     else:
         new_potential, own, *sends, tall_sum, whole, wide_part, rim = rest
     place = Place(where, *grid)
@@ -277,65 +300,60 @@
                 shared[r * cores_n + k] = sorted_codes[:, k * per_core : (k + 1) * per_core]
     else:
         new_potential[...] = updated
-    reconstruct(z, place, coding, dic, pixels, tall_sum, own, sends)
-
-
-def pack_kernel(z, grid, where, own, from_even, from_odd, packed, joined, flat):
-    joined[...] = own[...]
-    add_sides(z, Place(where, *grid), joined, (from_even, from_odd))
-    base = z.tall * z.cols
-    flat[base:, :] = jnp.zeros((z.packed - base, z.lanes), F32)
-    for p in range(z.tall):
-        flat[p * z.cols : (p + 1) * z.cols, :] = joined[p, 0 : z.cols, :]
-    for c in range(MARGIN):
-        start = base + c * z.tall_pad
-        flat[start : start + z.tall, :] = joined[:, z.cols + c, :]
-    half = z.packed // 2
-    packed[0 : z.packed, :] = flat[:, 0:128].astype(BF16)
-    tail = z.cell - 128
-    ends = jnp.concatenate([flat[0:half, 128 : z.cell], flat[half:, 128 : z.cell]], axis=1)
-    packed[z.packed :, 0 : 2 * tail] = ends.astype(BF16)
-
-
-def learn_kernel(z, groups, where, shared, packed, partial, flat, whole, wide_part, codes):
+    reconstruct(z, place, coding, dic, pixels, tall_sum, own)
+    if last:
+        send_all(z, place, own, flat, packed, outer)
+    else:
+        send_sides(z, place, own, sends)
+
+
+def learn_kernel(
+    z, grid, groups, where, shared, packed, partial, flat, joined, whole, wide_part, codes
+):
     rows_n, cores_n, _ = groups
     members = rows_n * cores_n
     stride = members * z.cols
     base = z.tall * z.cols
     half = z.packed // 2
     tail = z.cell - 128
-    row = where[0]
-
-    for k in range(cores_n):
-        for x in range(rows_n):
-            d = (row ^ x) if rows_n & (rows_n - 1) == 0 else (row + x) % rows_n
-            block = packed[k, x].astype(F32)
-            flat[d, :, 0:128] = block[0 : z.packed]
-            flat[d, 0:half, 128 : z.cell] = block[z.packed :, 0:tail]
-            flat[d, half:, 128 : z.cell] = block[z.packed :, tail : 2 * tail]
-        for r in range(rows_n):
+    end = z.packed + half
+    place = Place(where, *grid)
+
+    for x in range(rows_n):
+        d = (place.row ^ x) if rows_n & (rows_n - 1) == 0 else (place.row + x) % rows_n
+        for k in range(cores_n):
+            flat[:, 0:128] = packed[k, x, 0 : z.packed, :].astype(F32)
+            ends = packed[k, x, z.packed : end, :].astype(F32)
+            flat[0:half, 128 : z.cell] = ends[:, 0:tail]
+            flat[half:, 128 : z.cell] = ends[:, tail : 2 * tail]
+            joined[k, d, :, 0 : z.cols, :] = flat[0:base, :].reshape(z.tall, z.cols, z.lanes)
+            for c in range(MARGIN):
+                start = base + c * z.tall_pad
+                joined[k, d, :, z.cols + c, :] = flat[start : start + z.tall, :]
+        for c in range(MARGIN):
+            both = joined[0, d, :, z.cols + c, :] + joined[1, d, :, c, :]
+            joined[0, d, :, z.cols + c, :] = both
+            joined[1, d, :, c, :] = both
+        for k, first, there in ((0, 0, place.col > 1), (1, z.cols, place.col < place.cols_n - 2)):
+
+            @pl.when(there)
+            def _(x=x, d=d, k=k, first=first):
+                for c in range(MARGIN):
+                    start = end + 2 * c * z.tall_pad
+                    low = packed[k, x, start : start + z.tall_pad, :].astype(F32)
+                    start += z.tall_pad
+                    high = packed[k, x, start : start + z.tall_pad, :].astype(F32)
+                    joined[k, d, :, first + c, 0:128] += low[0 : z.tall]
+                    joined[k, d, :, first + c, 128 : z.cell] += high[0 : z.tall, 0:tail]
+
+    for r in range(rows_n):
+        for k in range(cores_n):
             d = r * cores_n + k
-            for source, low, high, at in (
-                (r, 0, z.tall, 0),
-                (r - 1, z.rows, z.tall, 0),
-                (r + 1, 0, MARGIN, z.rows),
-            ):
-                if not 0 <= source < rows_n:
-                    continue
-                n = high - low
-                main = flat[source, low * z.cols : high * z.cols, :].reshape(n, z.cols, z.lanes)
-                side = [
-                    flat[source, base + c * z.tall_pad + low : base + c * z.tall_pad + high, :]
-                    for c in range(MARGIN)
-                ]
-                if source == r:
-                    whole[at : at + n, 0 : z.cols, :] = main
-                    for c in range(MARGIN):
-                        whole[at : at + n, z.cols + c, :] = side[c]
-                else:
-                    whole[at : at + n, 0 : z.cols, :] += main
-                    for c in range(MARGIN):
-                        whole[at : at + n, z.cols + c, :] += side[c]
+            whole[...] = joined[k, r]
+            if r > 0:
+                whole[0:MARGIN] += joined[k, r - 1, z.rows :]
+            if r + 1 < rows_n:
+                whole[z.rows :] += joined[k, r + 1, 0:MARGIN]
             windows_of(z, whole, wide_part, d * z.cols, stride)
             for i in range(z.rows):
                 codes[i * stride + d * z.cols : i * stride + (d + 1) * z.cols, :] = shared[
@@ -403,6 +421,7 @@
     rim_v = pltpu.VMEM((z.rim, z.lanes), F32)
     tall_v = pltpu.VMEM((z.tall * z.cols, z.band), F32)
     wide_v = pltpu.VMEM((z.tall * z.cols, z.band), BF16)
+    flat_v = pltpu.VMEM((z.packed, z.lanes), F32)
     site_v = pltpu.VMEM((z.sites, atom_count), F32)
     outs = [own_v, side_v, side_v]
 
@@ -418,7 +437,7 @@
         (where, membrane.reshape(z.sites, atom_count), picture, dictionary),
         [
             tall_v,
-            pltpu.VMEM((3, z.rows * picture.shape[2], z.cell), BF16),
+            pltpu.VMEM((3 * picture.shape[2], z.cell), BF16),
             pltpu.VMEM(picture.shape, F32),
             pltpu.SemaphoreType.DMA((SPAN + 2,)),
         ],
@@ -437,38 +456,44 @@
         ends = swapped("row", rows_n, ends)
         final = [
             jax.ShapeDtypeStruct((z.sites, atom_count), F32),
-            *outs,
+            pltpu.VMEM((z.packed * 3 // 2, 128), BF16),
+            pltpu.VMEM((2 * MARGIN * z.tall_pad, 128), BF16),
             pltpu.VMEM((members, z.sites, atom_count // members), BF16),
         ]
-        potential, own, *rest = call(
+        potential, *rest = call(
             functools.partial(sweep_kernel, z, grid, last, groups),
             final if last else [site_v] + outs,
             (where, potential, joined, *ends, pixels, dic),
-            [tall_v, own_v, wide_v, rim_v],
+            [tall_v, own_v, wide_v, rim_v] + ([own_v, flat_v] if last else []),
             "sweep",
         )
-        sides = rest[:2]
+        if not last:
+            own, *sides = rest
     final_codes = potential.reshape(membrane.shape)
-    shared = lax.all_to_all(rest[2], ("row", "core"), 0, 0, tiled=True)
-    (packed,) = call(
-        functools.partial(pack_kernel, z, grid),
-        [pltpu.VMEM((z.packed * 3 // 2, 128), BF16)],
-        (where, own, *sideways(sides)),
-        [own_v, pltpu.VMEM((z.packed, z.lanes), F32)],
-        "pack",
-    )
-    blocks = [packed]
-    for x in range(1, rows_n):
+    packed, outer, shared = rest
+
+    def along_row(block):
         power = rows_n & (rows_n - 1) == 0
-        route = [(i ^ x if power else (i + x) % rows_n, i) for i in range(rows_n)]
-        blocks.append(lax.ppermute(packed, "row", route))
-    blocks = lax.all_gather(jnp.stack(blocks), "core", axis=0, tiled=False)
+        return [block] + [
+            lax.ppermute(
+                block, "row", [(i ^ x if power else (i + x) % rows_n, i) for i in range(rows_n)]
+            )
+            for x in range(1, rows_n)
+        ]
+
+    outer = lax.ppermute(outer, ("yx", "core"), partners(cols_n)[1])
+    packed = along_row(packed)
+    shared = lax.all_to_all(shared, ("row", "core"), 0, 0, tiled=True)
+    outer = along_row(outer)
+    blocks = jnp.stack([jnp.concatenate(b) for b in zip(packed, outer)])
+    blocks = lax.all_gather(blocks, "core", axis=0, tiled=False)
     (partial,) = call(
-        functools.partial(learn_kernel, z, groups),
+        functools.partial(learn_kernel, z, grid, groups),
         [pltpu.VMEM((atom_count // members, z.patch), BF16)],
         (where, shared, blocks),
         [
-            pltpu.VMEM((rows_n, z.packed, z.lanes), F32),
+            flat_v,
+            pltpu.VMEM((cores_n, rows_n, z.tall, z.wide_pad, z.lanes), F32),
             own_v,
             pltpu.VMEM((z.tall * members * z.cols, z.band), BF16),
             pltpu.VMEM((members * z.sites, atom_count // members), BF16),
@@ -488,10 +513,7 @@
 
 def solution(mesh):
     rows_n, cols_n = (mesh.shape["row"], mesh.shape["col"])
-    cores_n = 2 if cols_n % 2 == 0 else 1
-    split = Mesh(
-        mesh.devices.reshape(rows_n, cols_n // cores_n, cores_n), ("row", "yx", "core")
-    )
+    split = Mesh(mesh.devices.reshape(rows_n, cols_n // 2, 2), ("row", "yx", "core"))
     col = ("yx", "core")
     return jax.shard_map(
         shards,

time: 82.6 us -> 84.2 us (1.019)
  starting transfers between devices: 22.5 us -> 28 us
  waiting for transfers between devices: 20.9 us -> 18.2 us
  Pallas kernels: 21.3 us -> 20 us
    ppermute x3 -> x7, starting transfers between devices: 4.44 us -> 11.2 us  [the longest x6 10.3 us: along_row(): lax.ppermute(block, 'row', [(i ^ x if power else (i + x) % rows_n, i) for...]
    ppermute x10 -> x8, waiting for transfers between devices: 13.6 us -> 10.2 us  [swapped(): lax.ppermute(b, axis, route)]
    ppermute x10 -> x8, starting transfers between devices: 14.3 us -> 13 us  [swapped(): lax.ppermute(b, axis, route)]
    pallas_call x8 -> x7, Pallas kernels: 21.3 us -> 20 us  [call(): pl.pallas_call(kernel, out_shape=outs, in_specs=specs, out_specs=[VMEM] *...]
    ppermute x3 -> x7, waiting for transfers between devices: 7.29 us -> 7.92 us  [the longest x6 7.92 us: along_row(): lax.ppermute(block, 'row', [(i ^ x if power else (i + x) % rows_n, i) for...]
  transfers between devices with their start and end apart: 14 -> 16, of which waited for: 9 -> 7; matrix products, arithmetic and copies ran while one was open for 0% -> 0% of each run, Pallas kernels for 1% -> 0%
where the time goes in v3:
time: 84.2 us; the launch traced here: 83.9 us
  starting transfers between devices  28 us (33%)
  Pallas kernels  20 us (24%)
  waiting for transfers between devices  18.2 us (22%)
  blocking collectives  16.8 us (20%)
    pallas_call x7, Pallas kernels, call(): pl.pallas_call(kernel, out_shape=outs, in_specs=specs, out_specs=[VMEM] *...  20 us
    all_to_all x1, blocking collectives, shards(): lax.all_to_all(partial.reshape(yx_n, owned, z.patch), 'yx', 0, 0, tiled=T...  14.3 us
    ppermute x8, starting transfers between devices, swapped(): lax.ppermute(b, axis, route)  13 us
    ppermute x6, starting transfers between devices, along_row(): lax.ppermute(block, 'row', [(i ^ x if power else (i + x) % rows_n, i) for...  10.3 us
    ppermute x8, waiting for transfers between devices, swapped(): lax.ppermute(b, axis, route)  10.2 us
    ppermute x6, waiting for transfers between devices, along_row(): lax.ppermute(block, 'row', [(i ^ x if power else (i + x) % rows_n, i) for...  7.92 us
    all_to_all x1, starting transfers between devices, shards(): shared = lax.all_to_all(shared, ('row', 'core'), 0, 0, tiled=True)  3.75 us
    all_gather x1, blocking collectives, shards(): blocks = lax.all_gather(blocks, 'core', axis=0, tiled=False)  2.44 us
  transfers between devices with their start and end apart: 16, of which 7 were waited for; matrix products, arithmetic and copies ran while one was open for 0% of the time, Pallas kernels for 0%

profile of v3, /device:TPU:0, one launch (start us, length us, event | category | flops | bytes accessed | tf_op | source)
XLA Modules:
  0.0 83.9 jit_solution(15347706307765126197)
XLA Ops:
  0.6 0.1 pad_add_fusion.where
  0.7 4.4 %first.1 = (f32[11,24,256]{2,1,0:T(8,128)S(1)}, bf16[3,16,256]{2,1,0:T(8,128)(2,1)S(1)}, bf16[3,16,256]{2,1,0:T(8,128)(2,1)S(1)}, f32[128,192]{1,0:T(8,128)S(1)}...) custom-call(s32[2]{0:T(128)S(1)} %pad_add_fusion.where, ...), custom_call_target="tpu_custom_call" | custom-call | tf_op jit(solution)/shard_map/first/pallas_call | solution.py:390
  5.1 0.6 collective-permute-start
  5.7 3.5 %collective-permute-start.1 = (bf16[3,16,256]{2,1,0:T(8,128)(2,1)S(1)}, bf16[3,16,256]{2,1,0:T(8,128)(2,1)S(1)}, u32[]{:S(2)}, u32[]{:S(2)}) collective-permute-start(bf16[3,16,256]{2,1,0:T(8,128)(2,1)S(1)} %get-tuple-element.29), channel_id=1, source_target_pairs={{0,7},{1,2},{2,1},{3,4},{4,3},{5,6},{6,5},{7,0},{8,15},{9,10},{10,... | collective-permute-start | bytes 73736 | tf_op jit(solution)/shard_map/ppermute | solution.py:413
  9.2 1.5 %collective-permute-done.1.from_odd = bf16[3,16,256]{2,1,0:T(8,128)(2,1)S(1)} collective-permute-done((bf16[3,16,256]{2,1,0:T(8,128)(2,1)S(1)}, bf16[3,16,256]{2,1,0:T(8,128)(2,1)S(1)}, u32[]{:S(2)}, u32[]{:S(2)}) %collective-permute-start.1) | collective-permute-done | bytes 24608 | tf_op jit(solution)/shard_map/ppermute | solution.py:413
  10.7 0.6 side.2
  11.4 1.8 %collective-permute-start.2 = (bf16[64,256]{1,0:T(8,128)(2,1)S(1)}, bf16[64,256]{1,0:T(8,128)(2,1)S(1)}, u32[]{:S(2)}, u32[]{:S(2)}) collective-permute-start(bf16[64,256]{1,0:T(8,128)(2,1)S(1)} %get-tuple-element.31), channel_id=1, source_target_pairs={{0,8},{8,0},{16,24},{24,16},{1,9},{9,1},{17,25},{25,17},{2,10},{10... | collective-permute-start | bytes 98312 | tf_op jit(solution)/shard_map/ppermute | solution.py:413
  13.2 2.5 %collective-permute-start.3 = (bf16[64,256]{1,0:T(8,128)(2,1)S(1)}, bf16[64,256]{1,0:T(8,128)(2,1)S(1)}, u32[]{:S(2)}, u32[]{:S(2)}) collective-permute-start(bf16[64,256]{1,0:T(8,128)(2,1)S(1)} %get-tuple-element.32), channel_id=1, source_target_pairs={{0,24},{8,16},{16,8},{24,0},{1,25},{9,17},{17,9},{25,1},{2,26},{10... | collective-permute-start | bytes 98312 | tf_op jit(solution)/shard_map/ppermute | solution.py:413
  15.6 3.2 %collective-permute-done.3.from_odd = bf16[64,256]{1,0:T(8,128)(2,1)S(1)} collective-permute-done((bf16[64,256]{1,0:T(8,128)(2,1)S(1)}, bf16[64,256]{1,0:T(8,128)(2,1)S(1)}, u32[]{:S(2)}, u32[]{:S(2)}) %collective-permute-start.3) | collective-permute-done | bytes 32800 | tf_op jit(solution)/shard_map/ppermute | solution.py:413
  18.9 4.3 %sweep.2 = (f32[128,1024]{1,0:T(8,128)S(1)}, f32[11,24,256]{2,1,0:T(8,128)S(1)}, bf16[3,16,256]{2,1,0:T(8,128)(2,1)S(1)}, bf16[3,16,256]{2,1,0:T(8,128)(2,1)S(1)}) custom-call(s32[2]{0:T(128)S(1)} %pad_add_fusion.where, f32[128,1024]{1,0:T(8,128)S(1)} %get-tuple-element.26.potential, f32[11,24,256]{2,1,0:T(8,128)S(1)} %get-tuple-element.30.joined, ...), custom_call_target="tpu_custom_call" | custom-call | tf_op jit(solution)/shard_map/sweep/pallas_call | solution.py:390
  23.2 0.1 collective-permute-start.4
  23.3 2.0 %collective-permute-start.5 = (bf16[3,16,256]{2,1,0:T(8,128)(2,1)S(1)}, bf16[3,16,256]{2,1,0:T(8,128)(2,1)S(1)}, u32[]{:S(2)}, u32[]{:S(2)}) collective-permute-start(bf16[3,16,256]{2,1,0:T(8,128)(2,1)S(1)} %get-tuple-element.38), channel_id=1, source_target_pairs={{0,7},{1,2},{2,1},{3,4},{4,3},{5,6},{6,5},{7,0},{8,15},{9,10},{10,... | collective-permute-start | bytes 73736 | tf_op jit(solution)/shard_map/ppermute | solution.py:413
  25.3 2.2 %collective-permute-done.5.from_odd = bf16[3,16,256]{2,1,0:T(8,128)(2,1)S(1)} collective-permute-done((bf16[3,16,256]{2,1,0:T(8,128)(2,1)S(1)}, bf16[3,16,256]{2,1,0:T(8,128)(2,1)S(1)}, u32[]{:S(2)}, u32[]{:S(2)}) %collective-permute-start.5) | collective-permute-done | bytes 24608 | tf_op jit(solution)/shard_map/ppermute | solution.py:413
  27.5 0.6 side.3
  28.2 0.1 collective-permute-start.6
  28.2 2.5 %collective-permute-start.7 = (bf16[64,256]{1,0:T(8,128)(2,1)S(1)}, bf16[64,256]{1,0:T(8,128)(2,1)S(1)}, u32[]{:S(2)}, u32[]{:S(2)}) collective-permute-start(bf16[64,256]{1,0:T(8,128)(2,1)S(1)} %get-tuple-element.41), channel_id=1, source_target_pairs={{0,24},{8,16},{16,8},{24,0},{1,25},{9,17},{17,9},{25,1},{2,26},{10... | collective-permute-start | bytes 98312 | tf_op jit(solution)/shard_map/ppermute | solution.py:413
  30.8 1.4 %collective-permute-done.6.from_even = bf16[64,256]{1,0:T(8,128)(2,1)S(1)} collective-permute-done((bf16[64,256]{1,0:T(8,128)(2,1)S(1)}, bf16[64,256]{1,0:T(8,128)(2,1)S(1)}, u32[]{:S(2)}, u32[]{:S(2)}) %collective-permute-start.6) | collective-permute-done | bytes 32800 | tf_op jit(solution)/shard_map/ppermute | solution.py:413
  32.1 1.9 %collective-permute-done.7.from_odd = bf16[64,256]{1,0:T(8,128)(2,1)S(1)} collective-permute-done((bf16[64,256]{1,0:T(8,128)(2,1)S(1)}, bf16[64,256]{1,0:T(8,128)(2,1)S(1)}, u32[]{:S(2)}, u32[]{:S(2)}) %collective-permute-start.7) | collective-permute-done | bytes 32800 | tf_op jit(solution)/shard_map/ppermute | solution.py:413
  34.0 5.3 %sweep.3 = (f32[128,1024]{1,0:T(8,128)}, bf16[336,128]{1,0:T(8,128)(2,1)S(1)}, bf16[96,128]{1,0:T(8,128)(2,1)S(1)}, bf16[8,128,128]{2,1,0:T(8,128)(2,1)}) custom-call(s32[2]{0:T(128)S(1)} %pad_add_fusion.where, f32[128,1024]{1,0:T(8,128)S(1)} %get-tuple-element.35.potential, f32[11,24,256]{2,1,0:T(8,128)S(1)} %get-tuple-element.39.joined, ...), custom_call_target="tpu_custom_call" | custom-call | tf_op jit(solution)/shard_map/sweep/pallas_call | solution.py:390
  39.3 0.9 %collective-permute-start.8 = (bf16[96,128]{1,0:T(8,128)(2,1)S(1)}, bf16[96,128]{1,0:T(8,128)(2,1)S(1)}, u32[]{:S(2)}, u32[]{:S(2)}) collective-permute-start(bf16[96,128]{1,0:T(8,128)(2,1)S(1)} %get-tuple-element.45), channel_id=1, source_target_pairs={{0,7},{1,2},{2,1},{3,4},{4,3},{5,6},{6,5},{7,0},{8,15},{9,10},{10,... | collective-permute-start | bytes 73736 | tf_op jit(solution)/shard_map/ppermute | solution.py:484
  40.2 2.5 %collective-permute-start.13 = (bf16[336,128]{1,0:T(8,128)(2,1)S(1)}, bf16[336,128]{1,0:T(8,128)(2,1)S(1)}, u32[]{:S(2)}, u32[]{:S(2)}) collective-permute-start(bf16[336,128]{1,0:T(8,128)(2,1)S(1)} %get-tuple-element.44), channel_id=1, source_target_pairs={{24,0},{16,8},{8,16},{0,24},{25,1},{17,9},{9,17},{1,25},{26,2},{18... | collective-permute-start | bytes 258056 | tf_op jit(solution)/shard_map/ppermute | solution.py:478
  42.7 1.9 %collective-permute-start.9 = (bf16[336,128]{1,0:T(8,128)(2,1)S(1)}, bf16[336,128]{1,0:T(8,128)(2,1)S(1)}, u32[]{:S(2)}, u32[]{:S(2)}) collective-permute-start(bf16[336,128]{1,0:T(8,128)(2,1)S(1)} %get-tuple-element.44), channel_id=1, source_target_pairs={{8,0},{0,8},{24,16},{16,24},{9,1},{1,9},{25,17},{17,25},{10,2},{2,... | collective-permute-start | bytes 258056 | tf_op jit(solution)/shard_map/ppermute | solution.py:478
  44.6 3.8 %all-to-all-start = ((bf16[8,128,128]{2,1,0:T(8,128)(2,1)}), bf16[8,128,128]{2,1,0:T(8,128)(2,1)S(1)}, u32[]{:S(2)}, u32[]{:S(2)}) async-start(bf16[8,128,128]{2,1,0:T(8,128)(2,1)} %get-tuple-element.43), calls=%async_computation | async-start | bytes 524288 | tf_op jit(solution)/shard_map/all_to_all | solution.py:486
  48.4 3.8 %collective-permute-start.14 = (bf16[96,128]{1,0:T(8,128)(2,1)S(1)}, bf16[96,128]{1,0:T(8,128)(2,1)S(1)}, u32[]{:S(2)}, u32[]{:S(2)}) collective-permute-start(bf16[96,128]{1,0:T(8,128)(2,1)S(1)} %collective-permute-done.8), channel_id=1, source_target_pairs={{24,0},{16,8},{8,16},{0,24},{25,1},{17,9},{9,17},{1,25},{26,2},{18... | collective-permute-start | bytes 73736 | tf_op jit(solution)/shard_map/ppermute | solution.py:478
  52.2 6.2 %collective-permute-done.14 = bf16[96,128]{1,0:T(8,128)(2,1)S(1)} collective-permute-done((bf16[96,128]{1,0:T(8,128)(2,1)S(1)}, bf16[96,128]{1,0:T(8,128)(2,1)S(1)}, u32[]{:S(2)}, u32[]{:S(2)}) %collective-permute-start.14) | collective-permute-done | bytes 24608 | tf_op jit(solution)/shard_map/ppermute | solution.py:478
  58.4 2.1 %collective-permute-start.10 = (bf16[96,128]{1,0:T(8,128)(2,1)S(1)}, bf16[96,128]{1,0:T(8,128)(2,1)S(1)}, u32[]{:S(2)}, u32[]{:S(2)}) collective-permute-start(bf16[96,128]{1,0:T(8,128)(2,1)S(1)} %collective-permute-done.8), channel_id=1, source_target_pairs={{8,0},{0,8},{24,16},{16,24},{9,1},{1,9},{25,17},{17,25},{10,2},{2,... | collective-permute-start | bytes 73736 | tf_op jit(solution)/shard_map/ppermute | solution.py:478
  60.5 1.7 %collective-permute-done.10 = bf16[96,128]{1,0:T(8,128)(2,1)S(1)} collective-permute-done((bf16[96,128]{1,0:T(8,128)(2,1)S(1)}, bf16[96,128]{1,0:T(8,128)(2,1)S(1)}, u32[]{:S(2)}, u32[]{:S(2)}) %collective-permute-start.10) | collective-permute-done | bytes 24608 | tf_op jit(solution)/shard_map/ppermute | solution.py:478
  62.3 0.1 pad_maximum_fusion
  62.4 2.4 %all-gather = bf16[8,432,128]{2,1,0:T(8,128)(2,1)S(1)} all-gather(bf16[4,432,128]{2,1,0:T(8,128)(2,1)S(1)} %pad_maximum_fusion), channel_id=2, replica_groups=mesh['row'=4,'yx'=4,'core'=2] {'core'}, dimensions={0}, use_global_device_ids=true | all-gather | bytes 1327104 | tf_op jit(solution)/shard_map/all_gather | solution.py:489
  64.8 3.1 %learn.1 = bf16[128,3072]{1,0:T(8,128)(2,1)S(1)} custom-call(s32[2]{0:T(128)S(1)} %pad_add_fusion.where, bf16[8,128,128]{2,1,0:T(8,128)(2,1)S(1)} %all-to-all-done.shared, bf16[2,4,432,128]{3,2,1,0:T(8,128)(2,1)S(1)} %bitcast.14), custom_call_target="tpu_custom_call" | custom-call | tf_op jit(solution)/shard_map/learn/pallas_call | solution.py:390
  68.0 14.3 %all_to_all.10.parts = bf16[4,32,3072]{2,1,0:T(8,128)(2,1)S(1)} all-to-all(bf16[4,32,3072]{2,1,0:T(8,128)(2,1)S(1)} %bitcast.15), channel_id=1, replica_groups=mesh['row'=4,'yx'=4,'core'=2] {'yx'}, dimensions={0} | all-to-all | bytes 1572864 | tf_op jit(solution)/shard_map/all_to_all | solution.py:503
  82.3 1.6 %finish.1 = (f32[32,3072]{1,0:T(8,128)}, f32[32,3072]{1,0:T(8,128)}) custom-call(s32[2]{0:T(128)S(1)} %pad_add_fusion.where, bf16[4,32,3072]{2,1,0:T(8,128)(2,1)S(1)} %all_to_all.10.parts, f32[32,3072]{1,0:T(8,128)S(1)} %copy-done, bf16[32,3072]{1,0:T(8,128)(2,1)S(1)} %get-tuple-element.46.atoms), custom_call_target="tpu_custom_call" | custom-call | tf_op jit(solution)/shard_map/finish/pallas_call | solution.py:390
  (17 shorter events, 0.1 us)
Async XLA Ops:
  5.1 4.1 %collective-permute-start = (bf16[3,16,256]{2,1,0:T(8,128)(2,1)S(1)}, bf16[3,16,256]{2,1,0:T(8,128)(2,1)S(1)}, u32[]{:S(2)}, u32[]{:S(2)}) collective-permute-start(bf16[3,16,256]{2,1,0:T(8,128)(2,1)S(1)} %get-tuple-element.28), channel_id=1, source_target_pairs={{0,1},{1,0},{2,3},{3,2},{4,5},{5,4},{6,7},{7,6},{8,9},{9,8},{10,11... | collective-permute-start | bytes 73736 | tf_op jit(solution)/shard_map/ppermute | solution.py:413
  5.7 5.1 %collective-permute-start.1 = (bf16[3,16,256]{2,1,0:T(8,128)(2,1)S(1)}, bf16[3,16,256]{2,1,0:T(8,128)(2,1)S(1)}, u32[]{:S(2)}, u32[]{:S(2)}) collective-permute-start(bf16[3,16,256]{2,1,0:T(8,128)(2,1)S(1)} %get-tuple-element.29), channel_id=1, source_target_pairs={{0,7},{1,2},{2,1},{3,4},{4,3},{5,6},{6,5},{7,0},{8,15},{9,10},{10,... | collective-permute-start | bytes 73736 | tf_op jit(solution)/shard_map/ppermute | solution.py:413
  11.4 4.3 %collective-permute-start.2 = (bf16[64,256]{1,0:T(8,128)(2,1)S(1)}, bf16[64,256]{1,0:T(8,128)(2,1)S(1)}, u32[]{:S(2)}, u32[]{:S(2)}) collective-permute-start(bf16[64,256]{1,0:T(8,128)(2,1)S(1)} %get-tuple-element.31), channel_id=1, source_target_pairs={{0,8},{8,0},{16,24},{24,16},{1,9},{9,1},{17,25},{25,17},{2,10},{10... | collective-permute-start | bytes 98312 | tf_op jit(solution)/shard_map/ppermute | solution.py:413
  13.2 5.7 %collective-permute-start.3 = (bf16[64,256]{1,0:T(8,128)(2,1)S(1)}, bf16[64,256]{1,0:T(8,128)(2,1)S(1)}, u32[]{:S(2)}, u32[]{:S(2)}) collective-permute-start(bf16[64,256]{1,0:T(8,128)(2,1)S(1)} %get-tuple-element.32), channel_id=1, source_target_pairs={{0,24},{8,16},{16,8},{24,0},{1,25},{9,17},{17,9},{25,1},{2,26},{10... | collective-permute-start | bytes 98312 | tf_op jit(solution)/shard_map/ppermute | solution.py:413
  23.2 2.1 %collective-permute-start.4 = (bf16[3,16,256]{2,1,0:T(8,128)(2,1)S(1)}, bf16[3,16,256]{2,1,0:T(8,128)(2,1)S(1)}, u32[]{:S(2)}, u32[]{:S(2)}) collective-permute-start(bf16[3,16,256]{2,1,0:T(8,128)(2,1)S(1)} %get-tuple-element.37), channel_id=1, source_target_pairs={{0,1},{1,0},{2,3},{3,2},{4,5},{5,4},{6,7},{7,6},{8,9},{9,8},{10,11... | collective-permute-start | bytes 73736 | tf_op jit(solution)/shard_map/ppermute | solution.py:413
  23.3 4.2 %collective-permute-start.5 = (bf16[3,16,256]{2,1,0:T(8,128)(2,1)S(1)}, bf16[3,16,256]{2,1,0:T(8,128)(2,1)S(1)}, u32[]{:S(2)}, u32[]{:S(2)}) collective-permute-start(bf16[3,16,256]{2,1,0:T(8,128)(2,1)S(1)} %get-tuple-element.38), channel_id=1, source_target_pairs={{0,7},{1,2},{2,1},{3,4},{4,3},{5,6},{6,5},{7,0},{8,15},{9,10},{10,... | collective-permute-start | bytes 73736 | tf_op jit(solution)/shard_map/ppermute | solution.py:413
  28.2 4.0 %collective-permute-start.6 = (bf16[64,256]{1,0:T(8,128)(2,1)S(1)}, bf16[64,256]{1,0:T(8,128)(2,1)S(1)}, u32[]{:S(2)}, u32[]{:S(2)}) collective-permute-start(bf16[64,256]{1,0:T(8,128)(2,1)S(1)} %get-tuple-element.40), channel_id=1, source_target_pairs={{0,8},{8,0},{16,24},{24,16},{1,9},{9,1},{17,25},{25,17},{2,10},{10... | collective-permute-start | bytes 98312 | tf_op jit(solution)/shard_map/ppermute | solution.py:413
  28.2 5.8 %collective-permute-start.7 = (bf16[64,256]{1,0:T(8,128)(2,1)S(1)}, bf16[64,256]{1,0:T(8,128)(2,1)S(1)}, u32[]{:S(2)}, u32[]{:S(2)}) collective-permute-start(bf16[64,256]{1,0:T(8,128)(2,1)S(1)} %get-tuple-element.41), channel_id=1, source_target_pairs={{0,24},{8,16},{16,8},{24,0},{1,25},{9,17},{17,9},{25,1},{2,26},{10... | collective-permute-start | bytes 98312 | tf_op jit(solution)/shard_map/ppermute | solution.py:413
  34.0 48.3 %copy-start = (f32[32,3072]{1,0:T(8,128)S(1)}, f32[32,3072]{1,0:T(8,128)}, u32[]{:S(2)}) copy-start(f32[32,3072]{1,0:T(8,128)} %momentum.1) | copy-start | bytes 1179652
  39.3 9.1 %collective-permute-start.8 = (bf16[96,128]{1,0:T(8,128)(2,1)S(1)}, bf16[96,128]{1,0:T(8,128)(2,1)S(1)}, u32[]{:S(2)}, u32[]{:S(2)}) collective-permute-start(bf16[96,128]{1,0:T(8,128)(2,1)S(1)} %get-tuple-element.45), channel_id=1, source_target_pairs={{0,7},{1,2},{2,1},{3,4},{4,3},{5,6},{6,5},{7,0},{8,15},{9,10},{10,... | collective-permute-start | bytes 73736 | tf_op jit(solution)/shard_map/ppermute | solution.py:484
  40.2 20.3 %collective-permute-start.13 = (bf16[336,128]{1,0:T(8,128)(2,1)S(1)}, bf16[336,128]{1,0:T(8,128)(2,1)S(1)}, u32[]{:S(2)}, u32[]{:S(2)}) collective-permute-start(bf16[336,128]{1,0:T(8,128)(2,1)S(1)} %get-tuple-element.44), channel_id=1, source_target_pairs={{24,0},{16,8},{8,16},{0,24},{25,1},{17,9},{9,17},{1,25},{26,2},{18... | collective-permute-start | bytes 258056 | tf_op jit(solution)/shard_map/ppermute | solution.py:478
  42.7 17.8 %collective-permute-start.11 = (bf16[336,128]{1,0:T(8,128)(2,1)S(1)}, bf16[336,128]{1,0:T(8,128)(2,1)S(1)}, u32[]{:S(2)}, u32[]{:S(2)}) collective-permute-start(bf16[336,128]{1,0:T(8,128)(2,1)S(1)} %get-tuple-element.44), channel_id=1, source_target_pairs={{16,0},{24,8},{0,16},{8,24},{17,1},{25,9},{1,17},{9,25},{18,2},{26... | collective-permute-start | bytes 258056 | tf_op jit(solution)/shard_map/ppermute | solution.py:478
  42.7 19.6 %collective-permute-start.9 = (bf16[336,128]{1,0:T(8,128)(2,1)S(1)}, bf16[336,128]{1,0:T(8,128)(2,1)S(1)}, u32[]{:S(2)}, u32[]{:S(2)}) collective-permute-start(bf16[336,128]{1,0:T(8,128)(2,1)S(1)} %get-tuple-element.44), channel_id=1, source_target_pairs={{8,0},{0,8},{24,16},{16,24},{9,1},{1,9},{25,17},{17,25},{10,2},{2,... | collective-permute-start | bytes 258056 | tf_op jit(solution)/shard_map/ppermute | solution.py:478
  44.6 20.2 %all-to-all-start = ((bf16[8,128,128]{2,1,0:T(8,128)(2,1)}), bf16[8,128,128]{2,1,0:T(8,128)(2,1)S(1)}, u32[]{:S(2)}, u32[]{:S(2)}) async-start(bf16[8,128,128]{2,1,0:T(8,128)(2,1)} %get-tuple-element.43), calls=%async_computation | async-start | bytes 524288 | tf_op jit(solution)/shard_map/all_to_all | solution.py:486
  48.4 10.0 %collective-permute-start.14 = (bf16[96,128]{1,0:T(8,128)(2,1)S(1)}, bf16[96,128]{1,0:T(8,128)(2,1)S(1)}, u32[]{:S(2)}, u32[]{:S(2)}) collective-permute-start(bf16[96,128]{1,0:T(8,128)(2,1)S(1)} %collective-permute-done.8), channel_id=1, source_target_pairs={{24,0},{16,8},{8,16},{0,24},{25,1},{17,9},{9,17},{1,25},{26,2},{18... | collective-permute-start | bytes 73736 | tf_op jit(solution)/shard_map/ppermute | solution.py:478
  52.2 8.3 %collective-permute-start.12 = (bf16[96,128]{1,0:T(8,128)(2,1)S(1)}, bf16[96,128]{1,0:T(8,128)(2,1)S(1)}, u32[]{:S(2)}, u32[]{:S(2)}) collective-permute-start(bf16[96,128]{1,0:T(8,128)(2,1)S(1)} %collective-permute-done.8), channel_id=1, source_target_pairs={{16,0},{24,8},{0,16},{8,24},{17,1},{25,9},{1,17},{9,25},{18,2},{26... | collective-permute-start | bytes 73736 | tf_op jit(solution)/shard_map/ppermute | solution.py:478
  58.4 3.9 %collective-permute-start.10 = (bf16[96,128]{1,0:T(8,128)(2,1)S(1)}, bf16[96,128]{1,0:T(8,128)(2,1)S(1)}, u32[]{:S(2)}, u32[]{:S(2)}) collective-permute-start(bf16[96,128]{1,0:T(8,128)(2,1)S(1)} %collective-permute-done.8), channel_id=1, source_target_pairs={{8,0},{0,8},{24,16},{16,24},{9,1},{1,9},{25,17},{17,25},{10,2},{2,... | collective-permute-start | bytes 73736 | tf_op jit(solution)/shard_map/ppermute | solution.py:478
